TPU v7x, 32 devices: a whole 2x2x4 slice. The times are simulated.
32 devices in a mesh: ctx: 8 (over y, x, core), wsh: 4 (over z).
Axes of the slice: x: 2, y: 2, z: 4, core: 2. Of those that a mesh axis runs over, the one named last changes fastest.
Arguments:
- tokens: bfloat16 [4, 2048, 1088], P('wsh', 'ctx'), may hold values from -6 to 6
- seq_lengths: int32 [4, 5], P('wsh'), may hold values from 96 to 1280, as said below
- cotangent: bfloat16 [4, 2048, 1088], P('wsh', 'ctx'), may hold values from -6 to 6
- ln1_gain: bfloat16 [1088], P('wsh'), may hold values from 0.5 to 1.5
- ln1_bias: bfloat16 [1088], P('wsh'), may hold values from -1.25 to 1.25
- w_qkv: bfloat16 [1088, 3264], P('wsh'), may hold values from -0.1875 to 0.1875
- b_query: bfloat16 [1088], P('wsh'), may hold values from -1.75 to 1.75
- b_value: bfloat16 [1088], P('wsh'), may hold values from -0.625 to 0.625
- w_out: bfloat16 [1088, 1088], P('wsh'), may hold values from -0.375 to 0.375
- b_out: bfloat16 [1088], P('wsh'), may hold values from -1.25 to 1.25
- ln2_gain: bfloat16 [1088], P('wsh'), may hold values from 0.5 to 1.5
- ln2_bias: bfloat16 [1088], P('wsh'), may hold values from -1.25 to 1.25
- w_up: bfloat16 [1088, 4352], P('wsh'), may hold values from -0.1875 to 0.1875
- b_up: bfloat16 [4352], P('wsh'), may hold values from -1.75 to 1.75
- w_down: bfloat16 [4352, 1088], P('wsh'), may hold values from -0.09375 to 0.09375
- b_down: bfloat16 [1088], P('wsh'), may hold values from -1.25 to 1.25
Outputs:
- output: bfloat16 [4, 2048, 1088], P('wsh', 'ctx')
- grad_tokens: float32 [4, 2048, 1088], P('wsh', 'ctx')
- grad_ln1_gain: float32 [1088], P('wsh')
- grad_ln1_bias: float32 [1088], P('wsh')
- grad_w_qkv: float32 [1088, 3264], P('wsh')
- grad_b_query: float32 [1088], P('wsh')
- grad_b_value: float32 [1088], P('wsh')
- grad_w_out: float32 [1088, 1088], P('wsh')
- grad_b_out: float32 [1088], P('wsh')
- grad_ln2_gain: float32 [1088], P('wsh')
- grad_ln2_bias: float32 [1088], P('wsh')
- grad_w_up: float32 [1088, 4352], P('wsh')
- grad_b_up: float32 [4352], P('wsh')
- grad_w_down: float32 [4352, 1088], P('wsh')
- grad_b_down: float32 [1088], P('wsh')
Inputs may be any that keep to these rules, and one draw needn't show every extreme that they name: seq_lengths[g] holds group g's prompt length first, then the lengths of its 4 continuations, all positive; they sum to 2048 and the prompt is the longest.
All inputs are finite; a program needn't handle non-finite values.
Results may differ from a plain program's by a relative error of at most 0.018.
Values may be sent and summed in bfloat16 or wider, within the bound.
A program may use at most 320 MiB of HBM per device.

v0:
```python
import functools
import math

import jax
import jax.numpy as jnp
from jax import lax
from jax.experimental import pallas as pl
from jax.experimental.pallas import tpu as pltpu
from jax.sharding import PartitionSpec as P

D = 1088
HEADS = 17
HEAD_DIM = 64


def normalize(inputs):
    center = inputs - jnp.mean(inputs, -1, keepdims=True)
    inverse = lax.rsqrt(jnp.mean(center * center, -1, keepdims=True) + 1e-05)
    return (center * inverse, inverse)


def norm_back(grad_in, normed, inverse, gain):
    scaled = grad_in * gain
    return inverse * (
        scaled
        - jnp.mean(scaled, -1, keepdims=True)
        - normed * jnp.mean(scaled * normed, -1, keepdims=True)
    )


def rows_product(left, right):
    return lax.dot_general(
        left, right, (((0,), (0,)), ((), ())), preferred_element_type=jnp.float32
    )


def cols_product(left, right):
    return lax.dot_general(
        left, right, (((1,), (1,)), ((), ())), preferred_element_type=jnp.float32
    )


def sequence_ids(lengths, positions):
    bounds = jnp.cumsum(lengths)
    return jnp.sum((positions[:, None] >= bounds[None, :]).astype(jnp.int32), axis=1)


def allowed_pairs(lengths, query_pos, key_pos):
    query_owner = sequence_ids(lengths, query_pos)
    key_owner = sequence_ids(lengths, key_pos)
    return (key_pos[None, :] <= query_pos[:, None]) & (
        (key_owner[None, :] == 0) | (key_owner[None, :] == query_owner[:, None])
    )


def over_blocks(state_in, arrays, step_fn):
    total_rows = arrays[0].shape[0]
    block_rows = math.gcd(total_rows, 512)

    def advance(block_index, state_now):
        offset = block_index * block_rows
        pieces = tuple((lax.dynamic_slice_in_dim(array, offset, block_rows, 0) for array in arrays))
        return step_fn(state_now, pieces, offset)

    return lax.fori_loop(0, total_rows // block_rows, advance, state_in)


def sectioned_sum(partials):
    shares = lax.psum_scatter(partials, "wsh", scatter_dimension=0, tiled=True)
    return lax.psum(shares, "ctx")


def on_device(
    tokens,
    seq_lengths,
    cotangent,
    ln1_gain,
    ln1_bias,
    w_qkv,
    b_query,
    b_value,
    w_out,
    b_out,
    ln2_gain,
    ln2_bias,
    w_up,
    b_up,
    w_down,
    b_down,
):
    token_rows, grad_rows = (tokens[0], cotangent[0])
    shards = (
        w_qkv,
        w_out,
        w_up,
        w_down,
        b_query,
        b_value,
        b_out,
        b_up,
        b_down,
        ln1_gain,
        ln1_bias,
        ln2_gain,
        ln2_bias,
    )
    gathered = (
        lax.all_gather(shards[0], "wsh", axis=0, tiled=True),
        lax.all_gather(shards[1], "wsh", axis=0, tiled=True),
        lax.all_gather(shards[2], "wsh", axis=0, tiled=True),
        lax.all_gather(shards[3], "wsh", axis=0, tiled=True),
        lax.all_gather(shards[4], "wsh", axis=0, tiled=True),
        lax.all_gather(shards[5], "wsh", axis=0, tiled=True),
        lax.all_gather(shards[6], "wsh", axis=0, tiled=True),
        lax.all_gather(shards[7], "wsh", axis=0, tiled=True),
        lax.all_gather(shards[8], "wsh", axis=0, tiled=True),
        lax.all_gather(shards[9], "wsh", axis=0, tiled=True),
        lax.all_gather(shards[10], "wsh", axis=0, tiled=True),
        lax.all_gather(shards[11], "wsh", axis=0, tiled=True),
        lax.all_gather(shards[12], "wsh", axis=0, tiled=True),
    )
    qkv_full, out_full, up_full, down_full = (gathered[0], gathered[1], gathered[2], gathered[3])
    query_bias, value_bias, out_bias, up_bias, down_bias = [
        piece.astype(jnp.float32) for piece in gathered[4:9]
    ]
    gain_one, shift_one, gain_two, shift_two = [
        piece.astype(jnp.float32) for piece in gathered[9:13]
    ]
    lengths = seq_lengths[0]
    tok_rows = token_rows.shape[0]
    my_pos = lax.axis_index("ctx") * tok_rows + jnp.arange(tok_rows, dtype=jnp.int32)
    scale_qk = HEAD_DIM ** (-0.5)
    inputs = token_rows.astype(jnp.float32)
    normed_one, inverse_one = normalize(inputs)
    hidden_one = (normed_one * gain_one + shift_one).astype(jnp.bfloat16)
    joint_proj = jnp.dot(hidden_one, qkv_full, preferred_element_type=jnp.float32)
    queries = (joint_proj[:, :D] + query_bias).astype(jnp.bfloat16)
    key_rows = joint_proj[:, D : 2 * D].astype(jnp.bfloat16)
    value_rows = (joint_proj[:, 2 * D :] + value_bias).astype(jnp.bfloat16)
    query_heads = queries.reshape(tok_rows, HEADS, HEAD_DIM)
    my_key_heads = key_rows.reshape(tok_rows, HEADS, HEAD_DIM)
    my_value_heads = value_rows.reshape(tok_rows, HEADS, HEAD_DIM)

    def forward_step(state_now, pieces, first_row):
        key_heads = pieces[0].reshape(-1, HEADS, HEAD_DIM)
        value_heads = pieces[1].reshape(-1, HEADS, HEAD_DIM)
        key_pos = first_row + jnp.arange(key_heads.shape[0], dtype=jnp.int32)
        allowed = allowed_pairs(lengths, my_pos, key_pos)

        def forward_compute(inner):
            peak_old, total_old, accum_old = inner
            scores = (
                jnp.einsum(
                    "qhd,khd->hqk", query_heads, key_heads, preferred_element_type=jnp.float32
                )
                * scale_qk
            )
            scores = jnp.where(allowed[None], scores, -1e30)
            peak_new = jnp.maximum(peak_old, jnp.max(scores, -1))
            factor = jnp.exp(peak_old - peak_new)
            expos = jnp.where(allowed[None], jnp.exp(scores - peak_new[:, :, None]), 0.0)
            total_new = total_old * factor + jnp.sum(expos, -1)
            accum_new = accum_old * factor.T[:, :, None] + jnp.einsum(
                "hqk,khd->qhd",
                expos.astype(jnp.bfloat16),
                value_heads,
                preferred_element_type=jnp.float32,
            )
            return (peak_new, total_new, accum_new)

        return lax.cond(jnp.any(allowed), forward_compute, lambda inner: inner, state_now)

    start_state = (
        jnp.full((HEADS, tok_rows), -1e30, jnp.float32),
        jnp.zeros((HEADS, tok_rows), jnp.float32),
        jnp.zeros((tok_rows, HEADS, HEAD_DIM), jnp.float32),
    )
    peak, total, accum = over_blocks(
        start_state,
        (
            lax.all_gather(key_rows, "ctx", axis=0, tiled=True),
            lax.all_gather(value_rows, "ctx", axis=0, tiled=True),
        ),
        forward_step,
    )
    mixed = accum / total.T[:, :, None]
    log_sum = (peak + jnp.log(total)).T
    mixed_low = mixed.reshape(tok_rows, D).astype(jnp.bfloat16)
    middle = inputs + jnp.dot(mixed_low, out_full, preferred_element_type=jnp.float32) + out_bias
    normed_two, inverse_two = normalize(middle)
    hidden_two = (normed_two * gain_two + shift_two).astype(jnp.bfloat16)
    pre_act = jnp.dot(hidden_two, up_full, preferred_element_type=jnp.float32) + up_bias
    activ_low = jax.nn.gelu(pre_act, approximate=False).astype(jnp.bfloat16)
    result = middle + jnp.dot(activ_low, down_full, preferred_element_type=jnp.float32) + down_bias
    output_rows = result.astype(jnp.bfloat16)
    grad_top_f = grad_rows.astype(jnp.float32)
    grad_down = rows_product(activ_low, grad_rows)
    grad_down_bias = jnp.sum(grad_top_f, 0)
    grad_act = cols_product(grad_rows, down_full)
    cdf_part = 0.5 * (1.0 + lax.erf(pre_act * math.sqrt(0.5)))
    pdf_part = jnp.exp(-0.5 * pre_act * pre_act) / math.sqrt(2.0 * math.pi)
    grad_pre = (grad_act * (cdf_part + pre_act * pdf_part)).astype(jnp.bfloat16)
    grad_up = rows_product(hidden_two, grad_pre)
    grad_up_bias = jnp.sum(grad_pre.astype(jnp.float32), 0)
    grad_h2 = cols_product(grad_pre, up_full)
    grad_gain_two = jnp.sum(grad_h2 * normed_two, 0)
    grad_shift_two = jnp.sum(grad_h2, 0)
    grad_mid = grad_top_f + norm_back(grad_h2, normed_two, inverse_two, gain_two)
    grad_mid_low = grad_mid.astype(jnp.bfloat16)
    grad_out_w = rows_product(mixed_low, grad_mid_low)
    grad_out_bias = jnp.sum(grad_mid_low.astype(jnp.float32), 0)
    grad_mixed = cols_product(grad_mid_low, out_full).astype(jnp.bfloat16)
    grad_heads = grad_mixed.reshape(tok_rows, HEADS, HEAD_DIM)
    delta = jnp.sum(grad_heads.astype(jnp.float32) * mixed, -1)
    lse_all, delta_all = (
        lax.all_gather(log_sum, "ctx", axis=0, tiled=True),
        lax.all_gather(delta, "ctx", axis=0, tiled=True),
    )

    def query_step(state_now, pieces, first_row):
        key_heads = pieces[0].reshape(-1, HEADS, HEAD_DIM)
        value_heads = pieces[1].reshape(-1, HEADS, HEAD_DIM)
        key_pos = first_row + jnp.arange(key_heads.shape[0], dtype=jnp.int32)
        allowed = allowed_pairs(lengths, my_pos, key_pos)

        def query_compute(accum_old):
            scores = (
                jnp.einsum(
                    "qhd,khd->hqk", query_heads, key_heads, preferred_element_type=jnp.float32
                )
                * scale_qk
            )
            probs = jnp.where(allowed[None], jnp.exp(scores - log_sum.T[:, :, None]), 0.0)
            grad_probs = jnp.einsum(
                "qhd,khd->hqk", grad_heads, value_heads, preferred_element_type=jnp.float32
            )
            grad_scores = (probs * (grad_probs - delta.T[:, :, None])).astype(jnp.bfloat16)
            return accum_old + jnp.einsum(
                "hqk,khd->qhd", grad_scores, key_heads, preferred_element_type=jnp.float32
            )

        return lax.cond(jnp.any(allowed), query_compute, lambda inner: inner, state_now)

    zero_heads = jnp.zeros((tok_rows, HEADS, HEAD_DIM), jnp.float32)
    grad_query = over_blocks(
        zero_heads,
        (
            lax.all_gather(key_rows, "ctx", axis=0, tiled=True),
            lax.all_gather(value_rows, "ctx", axis=0, tiled=True),
        ),
        query_step,
    )

    def key_step(state_now, pieces, first_row):
        other_queries = pieces[0].reshape(-1, HEADS, HEAD_DIM)
        other_grads = pieces[1].reshape(-1, HEADS, HEAD_DIM)
        other_count = other_queries.shape[0]
        other_pos = first_row + jnp.arange(other_count, dtype=jnp.int32)
        other_lse = lax.dynamic_slice_in_dim(lse_all, first_row, other_count, 0)
        other_delta = lax.dynamic_slice_in_dim(delta_all, first_row, other_count, 0)
        allowed = allowed_pairs(lengths, other_pos, my_pos)

        def key_compute(inner):
            grad_key_old, grad_value_old = inner
            scores = (
                jnp.einsum(
                    "qhd,khd->hqk", other_queries, my_key_heads, preferred_element_type=jnp.float32
                )
                * scale_qk
            )
            probs = jnp.where(allowed[None], jnp.exp(scores - other_lse.T[:, :, None]), 0.0)
            grad_value_new = grad_value_old + jnp.einsum(
                "hqk,qhd->khd",
                probs.astype(jnp.bfloat16),
                other_grads,
                preferred_element_type=jnp.float32,
            )
            grad_probs = jnp.einsum(
                "qhd,khd->hqk", other_grads, my_value_heads, preferred_element_type=jnp.float32
            )
            grad_scores = (probs * (grad_probs - other_delta.T[:, :, None])).astype(jnp.bfloat16)
            grad_key_new = grad_key_old + jnp.einsum(
                "hqk,qhd->khd", grad_scores, other_queries, preferred_element_type=jnp.float32
            )
            return (grad_key_new, grad_value_new)

        return lax.cond(jnp.any(allowed), key_compute, lambda inner: inner, state_now)

    grad_key, grad_value = over_blocks(
        (zero_heads, zero_heads),
        (
            lax.all_gather(queries, "ctx", axis=0, tiled=True),
            lax.all_gather(grad_mixed, "ctx", axis=0, tiled=True),
        ),
        key_step,
    )
    grad_joint = jnp.concatenate(
        [
            (grad_query * scale_qk).reshape(tok_rows, D),
            (grad_key * scale_qk).reshape(tok_rows, D),
            grad_value.reshape(tok_rows, D),
        ],
        axis=1,
    ).astype(jnp.bfloat16)
    grad_qkv_w = rows_product(hidden_one, grad_joint)
    grad_joint_f = grad_joint.astype(jnp.float32)
    grad_query_bias = jnp.sum(grad_joint_f[:, :D], 0)
    grad_value_bias = jnp.sum(grad_joint_f[:, 2 * D :], 0)
    grad_h1 = cols_product(grad_joint, qkv_full)
    grad_gain_one = jnp.sum(grad_h1 * normed_one, 0)
    grad_shift_one = jnp.sum(grad_h1, 0)
    grad_input = grad_mid + norm_back(grad_h1, normed_one, inverse_one, gain_one)
    matrices = (grad_qkv_w, grad_out_w, grad_up, grad_down)
    vectors = (
        grad_query_bias,
        grad_value_bias,
        grad_out_bias,
        grad_up_bias,
        grad_down_bias,
        grad_gain_one,
        grad_shift_one,
        grad_gain_two,
        grad_shift_two,
    )
    totals = sectioned_sum(matrices + vectors)
    return (
        output_rows[None],
        grad_input[None],
        totals[9],
        totals[10],
        totals[0],
        totals[4],
        totals[5],
        totals[1],
        totals[6],
        totals[11],
        totals[12],
        totals[2],
        totals[7],
        totals[3],
        totals[8],
    )


SLOTS = 5
WIDE = 384
ROWS = 256
HALF = ROWS // 2
CHIPS = 4
TILE = 128
UP_ROWS, DOWN_ROWS = (144, 160)
MESH_ID = pl.DeviceIdType.MESH
F32, BF16 = (jnp.float32, jnp.bfloat16)
NEG = -1e30
HEAD_TABLE = ((0, 5, 9, 13, -40), (1, 6, 10, 14, -40), (2, 7, 11, 15, -40), (3, 4, 8, 12, 16))
B_QUERY, B_VALUE, B_OUT, B_DOWN, GAIN_1, SHIFT_1, GAIN_2, SHIFT_2, B_UP = range(9)


def nn(left, right):
    return jnp.dot(left, right, preferred_element_type=F32)


def remote(src, dst, send, recv, where):
    return pltpu.make_async_remote_copy(
        src_ref=src, dst_ref=dst, send_sem=send, recv_sem=recv, device_id=where, device_id_type=MESH_ID
    )


def rows16(start, size):
    return pl.ds(pl.multiple_of(start, 16), size)


class Place:
    def __init__(self):
        self.c, self.z = (lax.axis_index("ctx"), lax.axis_index("wsh"))
        self.t, self.p = (self.c // 2, self.c % 2)
        self.tx, self.ty, self.td = (self.flip(1, 0), self.flip(0, 1), self.flip(1, 1))

    def flip(self, dx, dy):
        return (self.t // 2 + dy) % 2 * 2 + (self.t % 2 + dx) % 2

    def chip(self, chip):
        return (chip * 2 + self.p, self.z)

    def twin(self):
        return (self.t * 2 + 1 - self.p, self.z)

    def plane(self, step):
        return (self.c, (self.z + step) % 4)

    def greet(self, planes=True):
        barrier = pltpu.get_barrier_semaphore()
        others = [self.chip(self.tx), self.chip(self.ty), self.twin()]
        if planes:
            others += [self.plane(1), self.plane(2), self.plane(3)]
        for where in others:
            pl.semaphore_signal(barrier, inc=1, device_id=where, device_id_type=MESH_ID)
        pl.semaphore_wait(barrier, len(others))


class Gather:
    def __init__(self, e, own, view, rows, cut, send, recv):
        self.e, self.own, self.view, self.send, self.recv = (e, own, view, send, recv)
        self.parts = (pl.ds(0, cut), pl.ds(cut, rows - cut))

    def copy(self, i):
        e = self.e
        chip = (e.t, e.t, e.t, e.t, e.tx, e.ty)[i]
        part = self.parts[(0, 1, 1, 0, 0, 1)[i]]
        src = self.own if i < 4 else self.view(chip)
        where = e.chip((e.tx, e.tx, e.ty, e.ty, e.ty, e.tx)[i])
        return remote(src.at[part], self.view(chip).at[part], self.send.at[i], self.recv.at[i], where)

    def start(self):
        for i in (0, 2, 1, 3):
            self.copy(i).start()

    def forward(self):
        self.copy(0).wait_recv()
        self.copy(4).start()
        self.copy(2).wait_recv()
        self.copy(5).start()

    def have_x(self):
        self.copy(1).wait_recv()

    def have_y(self):
        self.copy(3).wait_recv()

    def have_far(self):
        self.copy(4).wait_recv()
        self.copy(5).wait_recv()

    def sent(self):
        for i in range(6):
            self.copy(i).wait_send()


class Scatter:
    def __init__(self, e, part, land, send, recv):
        self.e, self.part, self.land, self.send, self.recv = (e, part, land, send, recv)

    def copy(self, i):
        e = self.e
        chip = (e.td, e.td, e.tx, e.tx, e.ty, e.ty)[i]
        part = pl.ds((0, HALF, 0, HALF, HALF, 0)[i], HALF)
        where = e.chip((e.tx, e.ty, e.tx, e.tx, e.ty, e.ty)[i])
        return remote(
            self.part.at[chip, part], self.land.at[i], self.send.at[i], self.recv.at[i], where
        )

    def far_ready(self):
        self.copy(0).start()
        self.copy(1).start()

    def x_ready(self):
        self.copy(2).start()

    def y_ready(self):
        self.copy(4).start()

    def relay(self):
        self.copy(1).wait_recv()
        chip = self.e.tx
        self.part[chip, HALF:] = (self.part[chip, HALF:].astype(F32) + self.land[1].astype(F32)).astype(BF16)
        self.copy(3).start()
        self.copy(0).wait_recv()
        chip = self.e.ty
        self.part[chip, :HALF] = (self.part[chip, :HALF].astype(F32) + self.land[0].astype(F32)).astype(BF16)
        self.copy(5).start()

    def total(self):
        for i in (2, 4, 3, 5):
            self.copy(i).wait_recv()
        first = self.land[2].astype(F32) + self.land[5].astype(F32)
        second = self.land[4].astype(F32) + self.land[3].astype(F32)
        return jnp.concatenate([first, second], 0)

    def sent(self):
        for i in range(6):
            self.copy(i).wait_send()


class ZGather:
    def __init__(self, e, own, held, send, recv, put):
        self.e, self.own, self.held, self.send, self.recv, self.put = (e, own, held, send, recv, put)

    def copy(self, way, j):
        e = self.e
        shard = e.z - j if way == 0 else e.z + j
        src = self.own if j == 0 else self.held.at[shard]
        return remote(
            src, self.held.at[shard], self.send.at[way, j], self.recv.at[way, j], e.plane(1 if way == 0 else 3)
        )

    def sends(self, way, j):
        z = self.e.z
        return (z < 3) & (z >= j) if way == 0 else (z > 0) & (z <= 3 - j)

    def step(self, j):
        z = self.e.z
        for way in range(2):
            if j > 0:
                @pl.when(z >= j if way == 0 else z <= 3 - j)
                def _():
                    self.copy(way, j - 1).wait_recv()
            if j < 3:
                @pl.when(self.sends(way, j))
                def _():
                    self.copy(way, j).start()
            if j > 0:
                @pl.when(z >= j if way == 0 else z <= 3 - j)
                def _():
                    self.put(z - j if way == 0 else z + j)

    def sent(self):
        for way in range(2):
            for j in range(3):
                @pl.when(self.sends(way, j))
                def _():
                    self.copy(way, j).wait_send()


class ZScatter:
    def __init__(self, e, own, staged, right, left, send, recv):
        self.e, self.own, self.staged, self.land = (e, own, staged, (right, left))
        self.send, self.recv = (send, recv)

    def copy(self, way, j, src):
        return remote(
            src, self.land[way].at[j], self.send.at[way, j], self.recv.at[way, j],
            self.e.plane(1 if way == 0 else 3),
        )

    def begin(self):
        for plane, way in ((0, 0), (3, 1)):
            @pl.when(self.e.z == plane)
            def _():
                for j in range(3):
                    self.copy(way, j, self.own.at[3 - j if way == 0 else j]).start()

    def relay(self, way, j):
        dest = 3 - j if way == 0 else j
        self.copy(way, j, self.staged.at[dest]).wait_recv()
        self.staged[dest] = (self.own[dest].astype(F32) + self.land[way][j].astype(F32)).astype(BF16)
        self.copy(way, j, self.staged.at[dest]).start()

    def first(self):
        for plane, way in ((1, 0), (2, 1)):
            @pl.when(self.e.z == plane)
            def _():
                self.relay(way, 0)

    def second(self):
        for plane, way in ((1, 0), (2, 1)):
            @pl.when(self.e.z == plane)
            def _():
                self.relay(1 - way, 0)
                self.relay(way, 1)

    def last(self, out):
        right, left = self.land
        for z in range(4):
            @pl.when(self.e.z == z)
            def _():
                total = self.own[z].astype(F32)
                if z > 0:
                    self.copy(0, 3 - z, self.own.at[z]).wait_recv()
                    total = total + right[3 - z].astype(F32)
                if z < 3:
                    self.copy(1, z, self.own.at[z]).wait_recv()
                    total = total + left[z].astype(F32)
                out[...] = total.astype(BF16)
                for way in range(2):
                    for j in range((3 - z) if way == 0 else z):
                        self.copy(way, j, self.own.at[z]).wait_send()


def dma(*shape):
    return pltpu.SemaphoreType.DMA(shape)


def params(number, mib=56):
    return pltpu.CompilerParams(
        collective_id=number, has_side_effects=True, vmem_limit_bytes=mib * 2**20
    )


def vmem(count):
    return [pl.BlockSpec(memory_space=pltpu.VMEM)] * count


class Halves:
    def __init__(self, e, whole, block, keep, step, local, send, recv):
        self.e, self.whole, self.block, self.keep, self.step = (e, whole, block, keep, step)
        self.local, self.send, self.recv = (local, send, recv)

    def copies(self, src, shard):
        e = self.e
        return (
            pltpu.make_async_copy(
                src, self.whole.at[rows16(shard * self.block + e.p * self.step, self.keep)], self.local.at[shard]
            ),
            remote(
                src.at[rows16(e.p * (self.keep - self.step), self.step)],
                self.whole.at[rows16(shard * self.block + e.p * self.keep, self.step)],
                self.send.at[shard], self.recv.at[shard], e.twin(),
            ),
        )

    def put(self, src, shard):
        for copy in self.copies(src, shard):
            copy.start()

    def wait(self, src):
        for shard in range(4):
            for copy in self.copies(src, shard):
                copy.wait()


def half_tiles(source, columns):
    def piece(column, side):
        if column is None:
            return jnp.zeros((source.shape[0], TILE), F32)
        start = column // TILE * TILE
        if start + TILE > source.shape[-1]:
            part = source[:, start : start + HEAD_DIM].astype(F32)
            tile = jnp.concatenate([part, jnp.zeros_like(part)], 1)
        else:
            tile = source[:, start : start + TILE].astype(F32)
        return tile if column % TILE // HEAD_DIM == side else pltpu.roll(tile, HEAD_DIM, 1)

    tiles = []
    for i in range(0, len(columns), 2):
        first, second = (piece(columns[i], 0), piece(columns[i + 1], 1))
        lane = lax.broadcasted_iota(jnp.int32, first.shape, 1)
        tiles.append(jnp.where(lane < HEAD_DIM, first, second))
    return tiles


def head_columns(heads, first):
    return [first + head * HEAD_DIM if head >= 0 else None for head in heads] + [None]


def project_kernel(
    x, cot, bias_0, bias_1, bias_2, bias_3, bias_4, bias_5, bias_6, bias_7, b_up, w_qkv, w_out, w_up, w_down,
    q_out, k_out, v_out, h_out, whole, out_w, vecs, halves, cot_out, x_out,
    qkv_rows, half, half_o, edge, held, held_o, raw, vec_in, vec_land, bias,
    v_send, v_recv, z_send, z_recv, a_send, a_recv, w_local, w_send, w_recv, kv_send, kv_recv, r_local,
):
    e = Place()
    t, p, z = (e.t, e.p, e.z)
    rows = pltpu.make_async_copy(w_qkv.at[rows16(p * TILE, 144)], qkv_rows, r_local.at[0])
    rows.start()
    loads = []
    for i in range(4):
        column = pl.multiple_of(D * i + HEAD_DIM * (i % 2) + 256 * t, TILE)
        loads.append((w_up.at[rows16(p * TILE, 144), pl.ds(column, 256)], halves.at[pl.ds(0, 144), pl.ds(256 * i, 256)]))
    column = pl.multiple_of(1024 + 2 * D * (t // 2), TILE)
    loads.append((w_up.at[rows16(p * TILE, 144), pl.ds(column, TILE)], edge))
    loads.append((w_down.at[rows16(HEAD_DIM * (z % 2) + 256 * t + TILE * p, TILE)], halves.at[pl.ds(144, TILE)]))
    loads.append((w_down.at[rows16(1024 * (1 - z % 2) + 32 * p, 32)], halves.at[pl.ds(272, 32)]))
    loads = [pltpu.make_async_copy(src, dst, r_local.at[1 + i]) for i, (src, dst) in enumerate(loads)]
    for copy in loads:
        copy.start()
    spot = lax.broadcasted_iota(jnp.int32, (D // 4, D), 1) - D // 4 * z
    match = (spot == lax.broadcasted_iota(jnp.int32, (D // 4, D), 0)).astype(F32).astype(BF16)
    biases = (bias_0, bias_1, bias_2, bias_3, bias_4, bias_5, bias_6, bias_7)
    biases = jnp.concatenate([ref[...].astype(F32).reshape(1, D // 4) for ref in biases], 0)
    vec_in[0] = nn(biases.astype(BF16), match)
    e.greet()

    def exchange(i):
        return [
            remote(vec_in.at[i], vec_land.at[k, i], v_send.at[i, k], v_recv.at[i, k], e.plane(k))
            for k in range(1, 4)
        ]

    vectors = exchange(0)
    for copy in vectors:
        copy.start()
    into = Halves(e, whole, 272, 144, 128, w_local.at[0], w_send.at[0], w_recv.at[0])
    into_o = Halves(e, raw, 80, 48, 32, w_local.at[1], w_send.at[1], w_recv.at[1])
    chain = ZGather(
        e, half, held, z_send.at[0], z_recv.at[0], lambda shard: into.put(held.at[shard], shard)
    )
    chain_o = ZGather(
        e, half_o, held_o, z_send.at[1], z_recv.at[1], lambda shard: into_o.put(held_o.at[shard], shard)
    )
    rows.wait()
    for chip in range(CHIPS):
        @pl.when(t == chip)
        def _():
            for a in range(3):
                tiles = half_tiles(qkv_rows, head_columns(HEAD_TABLE[chip], a * D))
                for i in range(3):
                    half[:, a * WIDE + i * TILE : a * WIDE + (i + 1) * TILE] = tiles[i].astype(BF16)

    chain.step(0)
    into.put(half, z)
    inputs = x[...].astype(F32).T
    x_out[...] = inputs.astype(BF16)
    normed, _ = normalize(inputs)
    total = vec_in[0]
    for k in range(1, 4):
        vectors[k - 1].wait_recv()
        total = total + vec_land[k, 0]
    vecs[:8] = total
    h_out[t] = (normed * vecs[GAIN_1 : GAIN_1 + 1] + vecs[SHIFT_1 : SHIFT_1 + 1]).astype(BF16)
    hidden = Gather(e, h_out.at[t], lambda chip: h_out.at[chip], ROWS, HALF, a_send, a_recv)
    hidden.start()
    ahead = (CHIPS - z) % CHIPS * 16
    for m in range(3):
        unit = 16 * (2 * p + m)
        late = jnp.where(unit < ahead, unit, 192 + unit)
        first = jnp.where(t < CHIPS - 1, ahead + HEAD_DIM * t + unit, late)
        half_o[16 * m : 16 * m + 16] = w_out[rows16(first, 16)]
    for chip in range(CHIPS):
        @pl.when(t == chip)
        def _():
            tiles = half_tiles(vecs, head_columns(HEAD_TABLE[chip], 0))
            for i in range(3):
                bias[:, i * TILE : (i + 1) * TILE] = tiles[i]

    spot = lax.broadcasted_iota(jnp.int32, (D, 320), 1)
    at = jnp.where(spot < 256, HEAD_DIM * (z % 2) + 256 * t + spot, 1024 * (1 - z % 2) + spot - 256)
    match = (lax.broadcasted_iota(jnp.int32, (D, 320), 0) == at).astype(F32).astype(BF16)
    ups = nn(b_up[...].astype(F32).reshape(1, D).astype(BF16), match)
    vec_in[1] = jnp.zeros((8, D), F32)
    for i in range(4):
        @pl.when(z == i)
        def _():
            vec_in[1, 0:1, 256 * i : 256 * i + 256] = ups[0:1, :256]

    @pl.when(z == t)
    def _():
        vec_in[1, 0:1, 1024:] = ups[0:1, 256:]

    vectors = vectors + exchange(1)
    for copy in vectors[3:]:
        copy.start()
    cot_out[:ROWS] = cot[...].astype(F32).T.astype(BF16)
    cot_out[ROWS:] = jnp.zeros((8, D), BF16)
    for copy in loads:
        copy.wait()
    column = edge[...].astype(F32)
    column = jnp.where(t % 2 == 1, pltpu.roll(column, HEAD_DIM, 1), column)
    halves[:144, 1024:] = column[:, :HEAD_DIM].astype(BF16)
    chain.step(1)
    hidden.forward()
    chain.step(2)
    chain_o.step(0)
    into_o.put(half_o, z)
    total = vec_in[1]
    for k in range(1, 4):
        vectors[2 + k].wait_recv()
        total = total + vec_land[k, 1]
    vecs[8:] = total
    chain.step(3)
    into.wait(half)

    def block(k, carry):
        src = e.flip((k + 1) // 2 % 2, k // 2)

        @pl.when(k == 1)
        def _():
            hidden.have_x()

        @pl.when(k == 2)
        def _():
            hidden.have_far()

        @pl.when(k == 3)
        def _():
            hidden.have_y()

        h = h_out[src]
        bias_q, bias_v = (bias[B_QUERY : B_QUERY + 1], bias[B_VALUE : B_VALUE + 1])
        q_out[src] = ((nn(h, whole[:, :WIDE]) + bias_q).astype(BF16) * 0.125).astype(BF16)
        mine = src * 2 + p
        k_out[mine] = nn(h, whole[:, WIDE : 2 * WIDE]).astype(BF16)
        remote(k_out.at[mine], k_out.at[mine], kv_send.at[k], kv_recv.at[k], e.twin()).start()
        v_out[mine] = (nn(h, whole[:, 2 * WIDE :]) + bias_v).astype(BF16)
        remote(
            v_out.at[mine], v_out.at[mine], kv_send.at[k + CHIPS], kv_recv.at[k + CHIPS], e.twin()
        ).start()
        return carry

    lax.fori_loop(0, CHIPS, block, 0)
    chain_o.step(1)
    chain_o.step(2)
    chain_o.step(3)
    into_o.wait(half_o)

    @pl.when(t == CHIPS - 1)
    def _():
        out_w[: SLOTS * HEAD_DIM] = raw[...]

    @pl.when(t < CHIPS - 1)
    def _():
        for i in range(4):
            out_w[i * HEAD_DIM : (i + 1) * HEAD_DIM] = raw[i * 80 : i * 80 + HEAD_DIM]
        out_w[4 * HEAD_DIM : 5 * HEAD_DIM] = jnp.zeros((HEAD_DIM, D), BF16)

    out_w[SLOTS * HEAD_DIM :] = jnp.zeros((WIDE - SLOTS * HEAD_DIM, D), BF16)
    for k in range(CHIPS):
        src = e.flip((k + 1) // 2 % 2, k // 2)
        other = src * 2 + 1 - p
        mine = src * 2 + p
        for ref, j in ((k_out, k), (v_out, k + CHIPS)):
            remote(ref.at[mine], ref.at[mine], kv_send.at[j], kv_recv.at[j], e.twin()).wait_send()
            remote(ref.at[other], ref.at[other], kv_send.at[j], kv_recv.at[j], e.twin()).wait_recv()
    for user in (hidden, chain, chain_o):
        user.sent()
    for copy in vectors:
        copy.wait_send()


def project(x, cot, biases, b_up, w_qkv, w_out, w_up, w_down):
    blocks = jax.ShapeDtypeStruct((CHIPS, ROWS, WIDE), BF16)
    keys = jax.ShapeDtypeStruct((2 * CHIPS, ROWS, WIDE), BF16)
    near, far = (vmem(1), [pl.BlockSpec(memory_space=pl.ANY)])
    return pl.pallas_call(
        project_kernel,
        out_shape=(
            blocks, keys, keys,
            jax.ShapeDtypeStruct((CHIPS, ROWS, D), BF16),
            jax.ShapeDtypeStruct((D, 3 * WIDE), BF16),
            jax.ShapeDtypeStruct((WIDE, D), BF16),
            jax.ShapeDtypeStruct((16, D), F32),
            jax.ShapeDtypeStruct((UP_ROWS + DOWN_ROWS, D), BF16),
            jax.ShapeDtypeStruct((ROWS + 8, D), BF16),
            jax.ShapeDtypeStruct((ROWS, D), BF16),
        ),
        in_specs=near * 11 + far + near + far * 2,
        out_specs=tuple(near * 10),
        scratch_shapes=[
            pltpu.VMEM((144, 3 * D), BF16),
            pltpu.VMEM((144, 3 * WIDE), BF16),
            pltpu.VMEM((48, D), BF16),
            pltpu.VMEM((144, TILE), BF16),
            pltpu.VMEM((4, 144, 3 * WIDE), BF16),
            pltpu.VMEM((4, 48, D), BF16),
            pltpu.VMEM((SLOTS * HEAD_DIM, D), BF16),
            pltpu.VMEM((2, 8, D), F32),
            pltpu.VMEM((4, 2, 8, D), F32),
            pltpu.VMEM((16, WIDE), F32),
            dma(2, 4), dma(2, 4), dma(2, 2, 3), dma(2, 2, 3), dma(6), dma(6),
            dma(2, 4), dma(2, 4), dma(2, 4), dma(2 * CHIPS), dma(2 * CHIPS), dma(8),
        ],
        compiler_params=params(1),
        name="project",
    )(x, cot, *biases, b_up, w_qkv, w_out, w_up, w_down)


def tile_bounds(lengths, block):
    ends = [lengths[0]]
    for i in range(1, 4):
        ends.append(ends[-1] + lengths[i])
    first = block * ROWS
    start_first = 0 * first
    for end in ends:
        start_first = jnp.where(first >= end, end, start_first)
    free = jnp.minimum(block, ends[0] // ROWS)
    resume = jnp.maximum(free + 1, start_first // ROWS)
    masked = jnp.where(free < block, 1 + jnp.maximum(block - resume, 0), 0)
    query_pos = first + lax.broadcasted_iota(jnp.int32, (1, ROWS), 1)
    start = jnp.zeros((1, ROWS), jnp.int32)
    for end in ends:
        start = jnp.where(query_pos >= end, end, start)
    return ends[0], query_pos, start, free, resume, masked


def visible(key_block, prompt, query_pos, start):
    key_pos = key_block * ROWS + lax.broadcasted_iota(jnp.int32, (ROWS, ROWS), 0)
    return (key_pos <= query_pos) & ((key_pos < prompt) | (key_pos >= start))


def half_of(rows, h):
    lane = lax.broadcasted_iota(jnp.int32, rows.shape, 1)
    return jnp.where((lane >= h * HEAD_DIM) & (lane < (h + 1) * HEAD_DIM), rows, jnp.zeros_like(rows))


def attend_kernel(lengths, parity, q, k, v, mixed, lse, turned):
    slab = pl.program_id(0)
    for j in range(2 * CHIPS):
        turned[j] = v[j].astype(F32).T.astype(BF16)

    def run(heads):
        def one(i, carry):
            block = 2 * i + parity[0]
            prompt, query_pos, start, free, resume, masked = tile_bounds(lengths, block)
            queries = [half_of(q[i], h) for h in heads]

            def tile(j, state, mask):
                keys = k[j]
                values = turned[j]
                new = []
                for h, (peak, total, accum) in zip(heads, state):
                    scores = cols_product(keys, queries[h])
                    if mask is not None:
                        scores = jnp.where(mask, scores, NEG)
                    peak_new = jnp.maximum(peak, jnp.max(scores, 0, keepdims=True))
                    factor = jnp.exp(peak - peak_new)
                    expos = jnp.exp(scores - peak_new)
                    total_new = total * factor + jnp.sum(expos, 0, keepdims=True)
                    part = values[h * HEAD_DIM : (h + 1) * HEAD_DIM]
                    accum_new = accum * factor + nn(part, expos.astype(BF16))
                    new.append((peak_new, total_new, accum_new))
                return tuple(new)

            state = tuple(
                (
                    jnp.full((1, ROWS), NEG, F32),
                    jnp.zeros((1, ROWS), F32),
                    jnp.zeros((HEAD_DIM, ROWS), F32),
                )
                for _ in heads
            )

            def other(m, s):
                j = jnp.where(m == 0, block, jnp.where(m == 1, free, resume + m - 2))
                return tile(j, s, visible(j, prompt, query_pos, start))

            state = lax.fori_loop(0, 1 + masked, other, state)
            state = lax.fori_loop(0, free, lambda j, s: tile(j, s, None), state)
            outs = []
            for h, (peak, total, accum) in zip(heads, state):
                outs.append(accum / total)
                lse[0, pl.ds(h * CHIPS + i, 1), :] = peak + jnp.log(total)
            if len(heads) == 1:
                outs.append(jnp.zeros((HEAD_DIM, ROWS), F32))
            mixed[i] = jnp.concatenate(outs, 0).T.astype(BF16)
            return carry

        lax.fori_loop(0, CHIPS, one, 0)

    @pl.when(slab < SLOTS // 2)
    def _():
        run((0, 1))

    @pl.when(slab >= SLOTS // 2)
    def _():
        lse[...] = jnp.zeros_like(lse)
        run((0,))


def slab_spec(count):
    return pl.BlockSpec((count, ROWS, 128), lambda s, *_: (0, 0, s))


def attend(lengths, parity, q, k, v):
    return pl.pallas_call(
        attend_kernel,
        out_shape=(
            jax.ShapeDtypeStruct((CHIPS, ROWS, WIDE), BF16),
            jax.ShapeDtypeStruct((3, 2 * CHIPS, ROWS), F32),
        ),
        grid_spec=pltpu.PrefetchScalarGridSpec(
            num_scalar_prefetch=2,
            grid=(3,),
            in_specs=[slab_spec(CHIPS), slab_spec(2 * CHIPS), slab_spec(2 * CHIPS)],
            out_specs=(
                slab_spec(CHIPS),
                pl.BlockSpec((1, 2 * CHIPS, ROWS), lambda s, *_: (s, 0, 0)),
            ),
            scratch_shapes=[pltpu.VMEM((2 * CHIPS, 128, ROWS), BF16)],
        ),
        compiler_params=pltpu.CompilerParams(vmem_limit_bytes=63 * 2**20),
        cost_estimate=pl.CostEstimate(flops=4 * 10**9, bytes_accessed=5 * 10**6, transcendentals=6 * 10**6),
        name="attend",
    )(lengths, parity, q, k, v)


def attend_back_kernel(
    lengths, parity, q, k, v, mixed, grad, lse, dq, dk, dv, turned, acc_k, acc_v
):
    slab = pl.program_id(0)
    for j in range(2 * CHIPS):
        turned[j] = k[j].astype(F32).T.astype(BF16)
    acc_k[...] = jnp.zeros_like(acc_k)
    acc_v[...] = jnp.zeros_like(acc_v)

    def run(heads):
        def one(i, carry):
            block = 2 * i + parity[0]
            prompt, query_pos, start, free, resume, masked = tile_bounds(lengths, block)
            queries = [half_of(q[i], h) for h in heads]
            grads = [half_of(grad[i], h) for h in heads]
            product = (grad[i].astype(F32) * mixed[i].astype(F32)).T
            deltas = [
                jnp.sum(product[h * HEAD_DIM : (h + 1) * HEAD_DIM], 0, keepdims=True) for h in heads
            ]
            sums = [lse[0, pl.ds(h * CHIPS + i, 1), :] for h in heads]

            def tile(j, state, mask):
                keys, values, keys_t = (k[j], v[j], turned[j])
                new = []
                add_k, add_v = (None, None)
                for h, accum in zip(heads, state):
                    scores = cols_product(keys, queries[h]) - sums[h]
                    if mask is not None:
                        scores = jnp.where(mask, scores, NEG)
                    probs = jnp.exp(scores)
                    grad_probs = cols_product(values, grads[h])
                    ds = (probs * (grad_probs - deltas[h])).astype(BF16)
                    part_v = nn(probs.astype(BF16), grads[h])
                    part_k = nn(ds, queries[h])
                    add_v = part_v if add_v is None else add_v + part_v
                    add_k = part_k if add_k is None else add_k + part_k
                    new.append(accum + nn(keys_t[h * HEAD_DIM : (h + 1) * HEAD_DIM], ds))
                acc_v[j] += add_v
                acc_k[j] += add_k
                return tuple(new)

            state = tuple(jnp.zeros((HEAD_DIM, ROWS), F32) for _ in heads)

            def other(m, s):
                j = jnp.where(m == 0, block, jnp.where(m == 1, free, resume + m - 2))
                return tile(j, s, visible(j, prompt, query_pos, start))

            state = lax.fori_loop(0, 1 + masked, other, state)
            state = list(lax.fori_loop(0, free, lambda j, s: tile(j, s, None), state))
            if len(heads) == 1:
                state.append(jnp.zeros((HEAD_DIM, ROWS), F32))
            dq[i] = (jnp.concatenate(state, 0) * 0.125).T.astype(BF16)
            return carry

        lax.fori_loop(0, CHIPS, one, 0)

    @pl.when(slab < SLOTS // 2)
    def _():
        run((0, 1))

    @pl.when(slab >= SLOTS // 2)
    def _():
        run((0,))

    dk[...] = acc_k[...].astype(BF16)
    dv[...] = acc_v[...].astype(BF16)


def attend_back(lengths, parity, q, k, v, mixed, grad, lse):
    few, many = (slab_spec(CHIPS), slab_spec(2 * CHIPS))
    return pl.pallas_call(
        attend_back_kernel,
        out_shape=(
            jax.ShapeDtypeStruct((CHIPS, ROWS, WIDE), BF16),
            jax.ShapeDtypeStruct((2 * CHIPS, ROWS, WIDE), BF16),
            jax.ShapeDtypeStruct((2 * CHIPS, ROWS, WIDE), BF16),
        ),
        grid_spec=pltpu.PrefetchScalarGridSpec(
            num_scalar_prefetch=2,
            grid=(3,),
            in_specs=[
                few, many, many, few, few,
                pl.BlockSpec((1, 2 * CHIPS, ROWS), lambda s, *_: (s, 0, 0)),
            ],
            out_specs=(few, many, many),
            scratch_shapes=[
                pltpu.VMEM((2 * CHIPS, 128, ROWS), BF16),
                pltpu.VMEM((2 * CHIPS, ROWS, 128), F32),
                pltpu.VMEM((2 * CHIPS, ROWS, 128), F32),
            ],
        ),
        compiler_params=pltpu.CompilerParams(vmem_limit_bytes=63 * 2**20),
        cost_estimate=pl.CostEstimate(flops=10 * 10**9, bytes_accessed=9 * 10**6, transcendentals=6 * 10**6),
        name="attend_back",
    )(lengths, parity, q, k, v, mixed, grad, lse)


def out_kernel(x, mixed, whole, vecs, middle, part, land, send, recv):
    e = Place()
    e.greet(planes=False)
    sums = Scatter(e, part, land, send, recv)

    def block(k, carry):
        dest = e.flip(1 - k // 2, 1 - k % 2)
        part[dest] = nn(mixed[dest], whole[...]).astype(BF16)

        @pl.when(k == 0)
        def _():
            sums.far_ready()

        @pl.when(k == 1)
        def _():
            sums.x_ready()

        @pl.when(k == 2)
        def _():
            sums.y_ready()

        return carry

    lax.fori_loop(0, CHIPS - 1, block, 0)
    total = x[...].astype(F32) + vecs[B_OUT : B_OUT + 1] + nn(mixed[e.t], whole[...])
    sums.relay()
    middle[...] = total + sums.total()
    sums.sent()


def out_project(x, mixed, whole, vecs):
    return pl.pallas_call(
        out_kernel,
        out_shape=jax.ShapeDtypeStruct((ROWS, D), F32),
        in_specs=vmem(4),
        out_specs=vmem(1)[0],
        scratch_shapes=[
            pltpu.VMEM((CHIPS, ROWS, D), BF16),
            pltpu.VMEM((6, HALF, D), BF16),
            dma(6), dma(6),
        ],
        compiler_params=params(2),
        name="out_project",
    )(x, mixed, whole, vecs)


def feed_kernel(
    middle, cot, cot_x, cot_y, cot_far, halves, vecs, out_w, mixed,
    to_x, to_y, to_far, out_own, grad_mid, gh_heads, g_out, g_down, share, sums, up_sum,
    up, down, lefts, rights, part_h, gmid, sum_h_land,
    full, grad_sum, land_up, land_down, land_more, g_up, staged, z_right, z_left, raw, land_out,
    a_send, a_recv, s_send, s_recv, w_local, w_send, w_recv, d_local, d_send, d_recv, g_send, g_recv, z_send, z_recv, c_local,
):
    e = Place()
    t, p = (e.t, e.p)
    hid, act, gpre, cots = (lefts.at[0], lefts.at[1], rights.at[0], rights.at[1])
    full_up, full_down = (full.at[0], full.at[1])
    e.greet()
    into = Halves(e, up, 272, 144, 128, w_local, w_send, w_recv)
    weights = []
    for i in range(4):
        weights.extend(into.copies(halves.at[i, pl.ds(0, 144)], i))
    for i in range(5):
        src = halves.at[i, pl.ds(144, TILE)] if i < 4 else halves.at[t, pl.ds(272, 32)]
        dst = down.at[rows16(256 * i + p * TILE, TILE) if i < 4 else rows16(1024 + p * 32, 32)]
        weights.append(pltpu.make_async_copy(src, dst, d_local.at[i]))
        weights.append(remote(src, dst, d_send.at[i], d_recv.at[i], e.twin()))
    for k, (ref, chip) in enumerate(((cot, t), (cot_x, e.tx), (cot_y, e.ty), (cot_far, e.td))):
        weights.append(pltpu.make_async_copy(ref.at[pl.ds(0, ROWS)], cots.at[chip], c_local.at[k]))
    for copy in weights:
        copy.start()
    normed, inverse = normalize(middle[...])
    hid[t] = (normed * vecs[GAIN_2 : GAIN_2 + 1] + vecs[SHIFT_2 : SHIFT_2 + 1]).astype(BF16)
    hidden = Gather(e, hid.at[t], lambda chip: hid.at[chip], ROWS, HALF, a_send.at[0], a_recv.at[0])
    hidden.start()
    sum_h = Scatter(e, part_h, sum_h_land, s_send, s_recv)
    for copy in weights:
        copy.wait()
    up_sum[...] = jnp.zeros_like(up_sum)

    def block(k, carry):
        src = e.flip((k + 1) // 2 % 2, k // 2)

        @pl.when(k == 1)
        def _():
            hidden.forward()
            hidden.have_x()

        @pl.when(k == 2)
        def _():
            hidden.have_far()

        @pl.when(k == 3)
        def _():
            hidden.have_y()

        pre = nn(hid[src], up[...]) + vecs[B_UP : B_UP + 1]
        cdf = 0.5 * (1.0 + lax.erf(pre * math.sqrt(0.5)))
        slope = cdf + pre * (jnp.exp(-0.5 * pre * pre) * (1.0 / math.sqrt(2.0 * math.pi)))
        act[src] = (pre * cdf).astype(BF16)
        grad = cols_product(cots[src], down[...]) * slope
        low = grad.astype(BF16)
        gpre[src] = low
        up_sum[...] += jnp.sum(low.astype(F32), 0, keepdims=True)
        part_h[src] = cols_product(low, up[...]).astype(BF16)

        @pl.when(k == 1)
        def _():
            sum_h.x_ready()

        @pl.when(k == 2)
        def _():
            sum_h.far_ready()

        @pl.when(k == 3)
        def _():
            sum_h.y_ready()

        return carry

    lax.fori_loop(0, CHIPS, block, 0)
    sum_h.relay()

    ups = [
        remote(
            full_up.at[rows16(i * 272 + (1 - p) * TILE, UP_ROWS)], land_up.at[i],
            g_send.at[0, i], g_recv.at[0, i], e.twin(),
        )
        for i in range(4)
    ]

    def matrices(i, carry):
        full[i] = rows_product(
            lefts[i].reshape(CHIPS * ROWS, D), rights[i].reshape(CHIPS * ROWS, D)
        ).astype(BF16)

        @pl.when(i == 0)
        def _():
            for copy in ups:
                copy.start()

        return carry

    lax.fori_loop(0, 2, matrices, 0)
    swaps = [
        remote(
            full_down.at[rows16(256 * i + (1 - p) * TILE, TILE)], land_down.at[i],
            g_send.at[1, i], g_recv.at[1, i], e.twin(),
        )
        for i in range(4)
    ]
    swaps.append(
        remote(
            full_down.at[rows16(1024 + (1 - p) * 32, 32)], land_more, g_send.at[2, 0], g_recv.at[2, 0], e.twin()
        )
    )
    for copy in swaps:
        copy.start()
    for copy in ups:
        copy.wait()
    for i in range(4):
        own = full_up[rows16(i * 272 + p * TILE, UP_ROWS)].astype(F32)
        g_up[i] = (own + land_up[i].astype(F32)).astype(BF16)
    planes = ZScatter(e, g_up, staged, z_right, z_left, z_send, z_recv)
    planes.begin()
    def outs(k, carry):
        rows = nn(act[e.flip(k % 2, k // 2)], down[...])
        for i, ref in enumerate((out_own, to_x, to_y, to_far)):
            @pl.when(k == i)
            def _():
                if i == 0:
                    ref[...] = middle[...] + vecs[B_DOWN : B_DOWN + 1] + rows
                else:
                    ref[:ROWS] = rows.astype(BF16)

        return carry

    lax.fori_loop(0, CHIPS, outs, 0)

    total = part_h[t].astype(F32) + sum_h.total()
    top = cot[:ROWS].astype(F32)
    grad_middle = top + norm_back(total, normed, inverse, vecs[GAIN_2 : GAIN_2 + 1])
    grad_mid[...] = grad_middle
    low = grad_middle.astype(BF16)
    gmid[t] = low
    spread = Gather(e, gmid.at[t], lambda chip: gmid.at[chip], ROWS, HALF, a_send.at[1], a_recv.at[1])
    spread.start()
    sums[0:1] = jnp.sum(low.astype(F32), 0, keepdims=True)
    sums[1:2] = jnp.sum(top, 0, keepdims=True)
    sums[2:3] = jnp.sum(total * normed, 0, keepdims=True)
    sums[3:4] = jnp.sum(total, 0, keepdims=True)
    sums[4:8] = jnp.zeros((4, D), F32)

    planes.first()
    for copy in swaps:
        copy.wait()
    more = (full_down[rows16(1024 + p * 32, 32)].astype(F32) + land_more[...].astype(F32)).astype(BF16)
    for i in range(4):
        own = full_down[rows16(256 * i + p * TILE, TILE)].astype(F32)
        g_down[i, :TILE] = (own + land_down[i].astype(F32)).astype(BF16)
        g_down[i, TILE:] = more
    spread.forward()
    planes.second()

    def heads(k, carry):
        src = e.flip((k + 1) // 2 % 2, k // 2)

        @pl.when(k == 1)
        def _():
            spread.have_x()

        @pl.when(k == 2)
        def _():
            spread.have_far()

        @pl.when(k == 3)
        def _():
            spread.have_y()

        rows = gmid[src]
        gh_heads[src] = cols_product(rows, out_w[...]).astype(BF16)
        grad_sum[...] += rows_product(mixed[src], rows)
        return carry

    grad_sum[...] = jnp.zeros_like(grad_sum)
    lax.fori_loop(0, CHIPS, heads, 0)
    grad_out = grad_sum[...].astype(BF16)

    @pl.when(t == CHIPS - 1)
    def _():
        raw[...] = grad_out[: SLOTS * HEAD_DIM]

    @pl.when(t < CHIPS - 1)
    def _():
        for i in range(4):
            raw[i * 80 : i * 80 + HEAD_DIM] = grad_out[i * HEAD_DIM : (i + 1) * HEAD_DIM]
            raw[i * 80 + HEAD_DIM : (i + 1) * 80] = jnp.zeros((16, D), BF16)

    swaps = [
        remote(
            raw.at[rows16(i * 80 + (1 - p) * 32, 48)], land_out.at[i], g_send.at[3, i], g_recv.at[3, i], e.twin()
        )
        for i in range(4)
    ]
    for copy in swaps:
        copy.start()
    for copy in swaps:
        copy.wait()
    for i in range(4):
        own = raw[rows16(i * 80 + p * 32, 48)].astype(F32)
        g_out[i] = (own + land_out[i].astype(F32)).astype(BF16)
    planes.last(share)
    for ref in (to_x, to_y, to_far):
        ref[ROWS:] = share[...]
    for user in (hidden, spread, sum_h):
        user.sent()


def feed(middle, cot, others, halves, vecs, out_w, mixed):
    blocks = pltpu.VMEM((CHIPS, ROWS, D), BF16)
    lands = pltpu.VMEM((6, HALF, D), BF16)
    matrix = pltpu.VMEM((D, D), BF16)
    mixture = jax.ShapeDtypeStruct((ROWS + UP_ROWS, D), BF16)
    return pl.pallas_call(
        feed_kernel,
        out_shape=(
            mixture, mixture, mixture,
            jax.ShapeDtypeStruct((ROWS, D), F32),
            jax.ShapeDtypeStruct((ROWS, D), F32),
            jax.ShapeDtypeStruct((CHIPS, ROWS, WIDE), BF16),
            jax.ShapeDtypeStruct((4, 48, D), BF16),
            jax.ShapeDtypeStruct((4, DOWN_ROWS, D), BF16),
            jax.ShapeDtypeStruct((UP_ROWS, D), BF16),
            jax.ShapeDtypeStruct((8, D), F32),
            jax.ShapeDtypeStruct((1, D), F32),
        ),
        in_specs=vmem(9),
        out_specs=tuple(vmem(11)),
        scratch_shapes=[matrix, matrix]
        + [pltpu.VMEM((2, CHIPS, ROWS, D), BF16)] * 2
        + [blocks] * 2
        + [lands, pltpu.VMEM((2, D, D), BF16), pltpu.VMEM((WIDE, D), F32)]
        + [
            pltpu.VMEM((4, UP_ROWS, D), BF16),
            pltpu.VMEM((4, TILE, D), BF16),
            pltpu.VMEM((32, D), BF16),
            pltpu.VMEM((4, UP_ROWS, D), BF16),
            pltpu.VMEM((4, UP_ROWS, D), BF16),
            pltpu.VMEM((3, UP_ROWS, D), BF16),
            pltpu.VMEM((3, UP_ROWS, D), BF16),
            pltpu.VMEM((SLOTS * HEAD_DIM, D), BF16),
            pltpu.VMEM((4, 48, D), BF16),
            dma(2, 6), dma(2, 6), dma(6), dma(6), dma(4), dma(4), dma(4),
            dma(5), dma(5), dma(5), dma(4, 4), dma(4, 4), dma(2, 3), dma(2, 3), dma(4),
        ],
        compiler_params=params(3, 63),
        name="feed",
    )(middle, cot, *others, halves, vecs, out_w, mixed)


def back_kernel(
    x, grad_mid, dq, dk, dv, hid, whole, vecs, share, from_x, from_y, from_far, share_down, out_own, g_out, sums, up_sum,
    output, grad_x, up_out, down_out, qkv_out, o_out, vec_out, b_up_out,
    joint, full, land, land_k, land_v, part, rows_own, sum_land, g_qkv, z_right, z_left, s_qkv,
    s_out, zo_right, zo_left, own_qkv, own_out, all_up, all_down, all_qkv, all_out, local, vec_land, totals, wide,
    kv_send, kv_recv, g_send, g_recv, s_send, s_recv, a_send, a_recv, z_send, z_recv, t_send, t_recv, v_send, v_recv, c_local,
):
    e = Place()
    t, p, z = (e.t, e.p, e.z)
    e.greet()
    swaps = []
    for k in range(CHIPS):
        chip = e.flip(1 - k // 2, 1 - k % 2)
        for j, (ref, dst) in enumerate(((dk, land_k), (dv, land_v))):
            swaps.append(
                remote(ref.at[chip * 2 + 1 - p], dst.at[chip], kv_send.at[j, k], kv_recv.at[j, k], e.twin())
            )
    for copy in swaps:
        copy.start()

    def spread(number, own, everything, rows, cut):
        return Gather(
            e, own, lambda chip: everything.at[p, chip], rows, cut, a_send.at[number], a_recv.at[number]
        )

    def hand(number, own, everything, k):
        chip = e.flip(k % 2, k // 2)
        src = own if k == 0 else everything.at[p, chip]
        return remote(
            src, everything.at[p, chip], t_send.at[number, k], t_recv.at[number, k], e.twin()
        )

    def handed(number, own, everything):
        for k in range(CHIPS):
            chip = e.flip(k % 2, k // 2)
            copy = remote(
                own, everything.at[1 - p, chip], t_send.at[number, k], t_recv.at[number, k], e.twin()
            )
            copy.wait_recv()
            copy.wait_send()

    feeds = [share] + [ref.at[pl.ds(ROWS, UP_ROWS)] for ref in (from_x, from_y, from_far)]
    keeps = []
    for k in range(CHIPS):
        slot = all_up.at[p, e.flip(k % 2, k // 2)]
        keeps.append(pltpu.make_async_copy(feeds[k], slot, c_local.at[k]))
    downs = spread(2, share_down, all_down, DOWN_ROWS, 80)
    downs.start()
    outs = ZScatter(e, g_out, s_out, zo_right, zo_left, z_send.at[0], z_recv.at[0])
    outs.begin()
    result = out_own[...]
    for ref in (from_x, from_y, from_far):
        result = result + ref[:ROWS].astype(F32)
    output[...] = result.T.astype(BF16)
    normed, inverse = normalize(x[...].astype(F32))
    local[...] = jnp.zeros_like(local)
    for k in range(CHIPS):
        joint[k, :, :WIDE] = dq[k]

    def trades(a):
        return [
            remote(
                full.at[a, rows16(i * 272 + (1 - p) * TILE, 144)], land.at[a, i],
                g_send.at[a, i], g_recv.at[a, i], e.twin(),
            )
            for i in range(4)
        ]

    def grads(a, carry):
        @pl.when(a == 1)
        def _():
            for copy in swaps:
                copy.wait()
            head_q, head_v = (jnp.zeros((1, WIDE), F32), jnp.zeros((1, WIDE), F32))
            for k in range(CHIPS):
                mine = k * 2 + p
                low_k = (dk[mine].astype(F32) + land_k[k].astype(F32)).astype(BF16)
                low_v = (dv[mine].astype(F32) + land_v[k].astype(F32)).astype(BF16)
                joint[k, :, WIDE : 2 * WIDE] = low_k
                joint[k, :, 2 * WIDE :] = low_v
                head_q = head_q + jnp.sum(dq[k].astype(F32), 0, keepdims=True)
                head_v = head_v + jnp.sum(low_v.astype(F32), 0, keepdims=True)
            local[pl.ds(12 + t, 1), :WIDE] = head_q
            local[pl.ds(12 + t, 1), WIDE : 2 * WIDE] = head_v
            outs.first()

        right = joint[:, :, pl.ds(pl.multiple_of(a * WIDE, TILE), WIDE)]
        full[a] = rows_product(
            hid[...].reshape(CHIPS * ROWS, D), right.reshape(CHIPS * ROWS, WIDE)
        ).astype(BF16)
        for copy in trades(a):
            copy.start()
        return carry

    lax.fori_loop(0, 3, grads, 0)
    downs.forward()
    outs.second()
    summed = Scatter(e, part, sum_land, s_send, s_recv)
    weights = ZScatter(e, g_qkv, s_qkv, z_right, z_left, z_send.at[1], z_recv.at[1])

    def block(k, carry):
        dest = e.flip(1 - k // 2, 1 - k % 2)
        value = cols_product(joint[dest], whole[...])

        @pl.when(k < 3)
        def _():
            part[dest] = value.astype(BF16)

        @pl.when(k == 0)
        def _():
            summed.far_ready()
            for a in range(3):
                for copy in trades(a):
                    copy.wait()
                for i in range(4):
                    own = full[a, rows16(i * 272 + p * TILE, 144)].astype(F32)
                    g_qkv[i, :, a * WIDE : (a + 1) * WIDE] = (own + land[a, i].astype(F32)).astype(BF16)
            weights.begin()

        @pl.when(k == 1)
        def _():
            summed.x_ready()

        @pl.when(k == 2)
        def _():
            summed.y_ready()

        @pl.when(k == 3)
        def _():
            rows_own[...] = value

        return carry

    lax.fori_loop(0, CHIPS, block, 0)
    outs.last(own_out)
    for k in range(CHIPS):
        keeps[k].start()
        slot = all_up.at[p, e.flip(k % 2, k // 2)]
        remote(feeds[k], slot, t_send.at[0, k], t_recv.at[0, k], e.twin()).start()
    hand(3, share_down, all_down, 0).start()
    all_down[p, t] = share_down[...]
    downs.have_x()
    downs.have_y()
    hand(3, share_down, all_down, 1).start()
    hand(3, share_down, all_down, 2).start()
    downs.have_far()
    hand(3, share_down, all_down, 3).start()
    weights.first()
    others = spread(0, own_out, all_out, 48, 32)
    others.start()
    all_out[p, t] = own_out[...]
    hand(1, own_out, all_out, 0).start()
    summed.relay()
    weights.second()
    total = rows_own[...] + summed.total()
    grad_x[...] = (grad_mid[...] + norm_back(total, normed, inverse, vecs[GAIN_1 : GAIN_1 + 1])).T
    local[:4] = sums[:4]
    local[4:5] = jnp.sum(total * normed, 0, keepdims=True)
    local[5:6] = jnp.sum(total, 0, keepdims=True)
    local[pl.ds(8 + t, 1), :] = up_sum[...]
    twin = remote(local, vec_land.at[0], v_send.at[0], v_recv.at[0], e.twin())
    twin.start()
    others.forward()
    others.have_x()
    others.have_y()
    hand(1, own_out, all_out, 1).start()
    hand(1, own_out, all_out, 2).start()
    others.have_far()
    hand(1, own_out, all_out, 3).start()
    twin.wait()
    totals[...] = local[...] + vec_land[0]
    planes = [
        remote(totals, vec_land.at[k], v_send.at[k], v_recv.at[k], e.plane(k)) for k in range(1, 4)
    ]
    for copy in planes:
        copy.start()
    weights.last(own_qkv)
    qkvs = spread(1, own_qkv, all_qkv, 144, 80)
    qkvs.start()
    hand(2, own_qkv, all_qkv, 0).start()
    all_qkv[p, t] = own_qkv[...]
    for copy in planes:
        copy.wait()
    local[...] = totals[...] + vec_land[1] + vec_land[2] + vec_land[3]
    chips = [
        remote(local, vec_land.at[3 + k], v_send.at[3 + k], v_recv.at[3 + k], e.chip(chip))
        for k, chip in ((1, e.tx), (2, e.ty), (3, e.td))
    ]
    for copy in chips:
        copy.start()

    handed(0, share, all_up)
    handed(3, share_down, all_down)
    for copy in keeps:
        copy.wait()
    for s in range(CHIPS):
        for q in range(2):
            rows = slice(q * TILE, q * TILE + 144)
            for i in range(4):
                column = D * i + HEAD_DIM * (i % 2) + 256 * s
                up_out[rows, column : column + 256] = all_up[q, s, :, 256 * i : 256 * (i + 1)]
            down_out[rows16(z % 2 * 64 + 256 * s + TILE * q, TILE)] = all_down[q, s, :TILE]
    for q in range(2):
        rows = slice(q * TILE, q * TILE + 144)
        for s in range(0, CHIPS, 2):
            pair = [all_up[q, s + i, :, 1024:].astype(F32) for i in range(2)]
            column = D * s + 1024
            up_out[rows, column : column + TILE] = jnp.concatenate(pair, 1).astype(BF16)
        down_out[rows16((1 - z % 2) * 1024 + 32 * q, 32)] = all_down[q, z, TILE:]

    handed(1, own_out, all_out)
    ahead = (CHIPS - z) % CHIPS * 16
    for s in range(CHIPS - 1):
        o_out[rows16(ahead + HEAD_DIM * s, 48)] = all_out[0, s]
        o_out[rows16(ahead + HEAD_DIM * s + 32, 32)] = all_out[1, s, :32]
    for u in range(SLOTS):
        q, first = ((0, 16 * u) if u < 3 else (1, 16 * u - 32))
        strip = all_out[q, CHIPS - 1, first : first + 16]

        @pl.when(16 * u < ahead)
        def _():
            o_out[16 * u : 16 * u + 16] = strip

        @pl.when(16 * u >= ahead)
        def _():
            o_out[192 + 16 * u : 208 + 16 * u] = strip

    qkvs.forward()
    qkvs.have_x()
    qkvs.have_y()
    hand(2, own_qkv, all_qkv, 1).start()
    hand(2, own_qkv, all_qkv, 2).start()
    qkvs.have_far()
    hand(2, own_qkv, all_qkv, 3).start()
    for copy in chips:
        copy.wait()
    totals[...] = local[...] + vec_land[4] + vec_land[5] + vec_land[6]
    wide[...] = jnp.zeros_like(wide)
    wide[:6, :D] = totals[:6]
    columns = {}
    for s, heads in enumerate(HEAD_TABLE):
        for slot, head in enumerate(heads):
            columns[head] = (s, slot * HEAD_DIM)
    lane = lax.broadcasted_iota(jnp.int32, (1, TILE), 1)
    for a in range(2):
        def span(head, side):
            s, column = columns[head]
            start = (column + a * WIDE) // TILE * TILE
            tile = totals[12 + s : 13 + s, start : start + TILE]
            return tile if column % TILE // HEAD_DIM == side else pltpu.roll(tile, HEAD_DIM, 1)

        for head in range(0, HEADS, 2):
            tile = span(head, 0)
            if head + 1 < HEADS:
                tile = jnp.where(lane < HEAD_DIM, tile, span(head + 1, 1))
            wide[6 + a : 7 + a, head * HEAD_DIM : head * HEAD_DIM + TILE] = tile
    for i in range(4):
        @pl.when(z == i)
        def _():
            row = wide[...]
            if i > 0:
                row = pltpu.roll(row, 9 * TILE - D // 4 * i, 1)
            vec_out[...] = row[:, :WIDE]
            pieces = [totals[8 + s : 9 + s, 256 * i : 256 * i + 256] for s in range(CHIPS)]
            more = totals[8 + i : 9 + i, 1024:]
            if i % 2 == 0:
                b_up_out[...] = jnp.concatenate(pieces + [more, more], 1)
            else:
                b_up_out[...] = pltpu.roll(jnp.concatenate(pieces + [more, more], 1), HEAD_DIM, 1)

    handed(2, own_qkv, all_qkv)
    source = {}
    for s, heads in enumerate(HEAD_TABLE):
        for slot, head in enumerate(heads):
            if head >= 0:
                for a in range(3):
                    source[a * HEADS + head] = (s, a * WIDE + slot * HEAD_DIM)
    for q in range(2):
        rows = slice(q * TILE, q * TILE + 144)

        def piece(g, side):
            s, column = source[g]
            tile = all_qkv[q, s, :, column // TILE * TILE : column // TILE * TILE + TILE].astype(F32)
            return tile if column % TILE // HEAD_DIM == side else pltpu.roll(tile, HEAD_DIM, 1)

        left = lax.broadcasted_iota(jnp.int32, (144, TILE), 1) < HEAD_DIM
        for g in range(0, 3 * HEADS - 1, 2):
            column = g * HEAD_DIM
            qkv_out[rows, column : column + TILE] = jnp.where(left, piece(g, 0), piece(g + 1, 1)).astype(BF16)
        column = (3 * HEADS - 1) * HEAD_DIM
        qkv_out[rows, column : column + HEAD_DIM] = piece(3 * HEADS - 1, 0)[:, :HEAD_DIM].astype(BF16)
    for user in (downs, others, qkvs, summed):
        user.sent()


def back(x, grad_mid, dq, dk, dv, hid, whole, vecs, share, others, share_down, out_own, g_out, sums, up_sum):
    heads = pltpu.VMEM((CHIPS, ROWS, WIDE), BF16)
    qkv, out = ((144, 3 * WIDE), (48, D))

    def many(count, shape):
        return pltpu.VMEM((count, *shape), BF16)

    return pl.pallas_call(
        back_kernel,
        out_shape=(
            jax.ShapeDtypeStruct((D, ROWS), BF16),
            jax.ShapeDtypeStruct((D, ROWS), F32),
            jax.ShapeDtypeStruct((D // 4, 4 * D), BF16),
            jax.ShapeDtypeStruct((D, D), BF16),
            jax.ShapeDtypeStruct((D // 4, 3 * D), BF16),
            jax.ShapeDtypeStruct((D // 4, D), BF16),
            jax.ShapeDtypeStruct((8, WIDE), F32),
            jax.ShapeDtypeStruct((1, 9 * TILE), F32),
        ),
        in_specs=vmem(17),
        out_specs=tuple(vmem(8)),
        scratch_shapes=[
            pltpu.VMEM((CHIPS, ROWS, 3 * WIDE), BF16),
            pltpu.VMEM((3, D, WIDE), BF16),
            pltpu.VMEM((3, 4, 144, WIDE), BF16),
            heads, heads,
            pltpu.VMEM((CHIPS, ROWS, D), BF16),
            pltpu.VMEM((ROWS, D), F32),
            pltpu.VMEM((6, HALF, D), BF16),
            many(4, qkv), many(3, qkv), many(3, qkv), many(4, qkv),
            many(4, out), many(3, out), many(3, out),
            pltpu.VMEM(qkv, BF16), pltpu.VMEM(out, BF16),
            pltpu.VMEM((2, CHIPS, UP_ROWS, D), BF16),
            pltpu.VMEM((2, CHIPS, DOWN_ROWS, D), BF16),
            pltpu.VMEM((2, CHIPS, *qkv), BF16),
            pltpu.VMEM((2, CHIPS, *out), BF16),
            pltpu.VMEM((16, D), F32),
            pltpu.VMEM((7, 16, D), F32),
            pltpu.VMEM((16, D), F32),
            pltpu.VMEM((8, 9 * TILE), F32),
            dma(2, CHIPS), dma(2, CHIPS), dma(3, 4), dma(3, 4), dma(6), dma(6), dma(3, 6), dma(3, 6),
            dma(2, 2, 3), dma(2, 2, 3), dma(4, 4), dma(4, 4), dma(7), dma(7), dma(4),
        ],
        compiler_params=params(4, 63),
        name="back",
    )(x, grad_mid, dq, dk, dv, hid, whole, vecs, share, *others, share_down, out_own, g_out, sums, up_sum)


def plane_device(
    tokens, seq_lengths, cotangent, ln1_gain, ln1_bias, w_qkv, b_query, b_value, w_out, b_out,
    ln2_gain, ln2_bias, w_up, b_up, w_down, b_down,
):
    c = lax.axis_index("ctx")
    lengths = seq_lengths[0]
    parity = (c % 2)[None].astype(jnp.int32)
    shard = D // 4

    biases = (b_query, b_value, b_out, b_down, ln1_gain, ln1_bias, ln2_gain, ln2_bias)
    q, k, v, hid, whole, out_w, vecs, halves, sent, x = project(
        tokens[0].T, cotangent[0].T, biases, b_up, w_qkv, w_out, w_up, w_down
    )
    halves = lax.all_gather(halves, "wsh", axis=0)

    def from_chips(*arrays):
        return [lax.ppermute(array, "ctx", list(enumerate(to))) for array, to in zip(arrays, flips)]

    flips = [[(i // 2 ^ mask) * 2 + i % 2 for i in range(2 * CHIPS)] for mask in (1, 2, 3)]
    tops = from_chips(sent, sent, sent)
    mixed, lse = attend(lengths, parity, q, k, v)
    middle = out_project(x, mixed, out_w, vecs)
    to_x, to_y, to_far, out_own, grad_mid, grad_heads, g_out, g_down, share, sums, up_sum = feed(
        middle, sent, tops, halves, vecs, out_w, mixed
    )
    others = from_chips(to_x, to_y, to_far)
    share_down = lax.psum_scatter(
        g_down.reshape(4 * DOWN_ROWS, D), "wsh", scatter_dimension=0, tiled=True
    )
    dq, dk, dv = attend_back(lengths, parity, q, k, v, mixed, grad_heads, lse)
    output, grad_x, grad_up, grad_down, grad_qkv, grad_out, vectors, grad_b_up = back(
        x, grad_mid, dq, dk, dv, hid, whole, vecs, share, others, share_down, out_own, g_out, sums, up_sum
    )
    grad_up, grad_down, grad_qkv, grad_out = (
        array.astype(F32) for array in (grad_up, grad_down, grad_qkv, grad_out)
    )

    mine = [row[:shard] for row in vectors]
    grad_b_up = grad_b_up[0, :D]
    return (
        output.T[None], grad_x.T[None],
        mine[4], mine[5], grad_qkv, mine[6], mine[7], grad_out, mine[0],
        mine[2], mine[3], grad_up, grad_b_up, grad_down, mine[1],
    )


def solution(mesh):
    in_specs = (
        P("wsh", "ctx", None),
        P("wsh", None),
        P("wsh", "ctx", None),
        P("wsh"),
        P("wsh"),
        P("wsh", None),
        P("wsh"),
        P("wsh"),
        P("wsh", None),
        P("wsh"),
        P("wsh"),
        P("wsh"),
        P("wsh", None),
        P("wsh"),
        P("wsh", None),
        P("wsh"),
    )
    out_specs = (
        P("wsh", "ctx", None),
        P("wsh", "ctx", None),
        P("wsh"),
        P("wsh"),
        P("wsh", None),
        P("wsh"),
        P("wsh"),
        P("wsh", None),
        P("wsh"),
        P("wsh"),
        P("wsh"),
        P("wsh", None),
        P("wsh"),
        P("wsh", None),
        P("wsh"),
    )
    sizes = (mesh.shape["ctx"], mesh.shape["wsh"])
    body = plane_device if sizes == (2 * CHIPS, 4) else on_device
    return jax.shard_map(
        body, mesh=mesh, in_specs=in_specs, out_specs=out_specs, check_vma=False
    )
```

profile of v0, /device:TPU:0, one launch (start us, length us, event | category | flops | bytes accessed | tf_op | source)
XLA Modules:
  0.0 348.1 jit_solution(12950593308110975683)
XLA Ops:
  7.2 51.2 %project.1 = (bf16[4,256,384]{2,1,0:T(8,128)(2,1)}, bf16[8,256,384]{2,1,0:T(8,128)(2,1)}, bf16[8,256,384]{2,1,0:T(8,128)(2,1)}, bf16[4,256,1088]{2,1,0:T(8,128)(...) custom-call(bf16[1088,256]{1,0:T(8,128)(2,1)} %bitcast.19, ...), custom_call_target="tpu_custom_call" | custom-call | tf_op jit(solution)/shard_map/project/pallas_call | solution.py:823
  58.7 2.5 collective-permute-start.2
  61.2 0.5 collective-permute-start.1
  61.7 0.5 collective-permute-start
  62.2 34.7 %attend.1 = (bf16[4,256,384]{2,1,0:T(8,128)(2,1)}, f32[3,8,256]{2,1,0:T(8,128)}) custom-call(s32[5]{0:T(128)} %bitcast.22, s32[1]{0:T(128)} %bitcast.5.parity, bf16[4,256,384]{2,1,0:T(8,128)(2,1)} %get-tuple-element.50.q, bf16[8,256,384]{2,1,0:T(8,128)(2,1)} %get-tuple-element.51.k, bf16[8,256,384]{2,1,0:T(8,128)(2,1)} %get-tuple-element.52.v), custom_call_target="tpu_custom_call" | custom-call | flops 4000000000 | bytes 5000000 | tf_op jit(solution)/shard_map/attend/pallas_call | solution.py:953
  96.9 31.8 %out_project.1.middle = f32[256,1088]{1,0:T(8,128)} custom-call(bf16[256,1088]{1,0:T(8,128)(2,1)} %get-tuple-element.49.x, bf16[4,256,384]{2,1,0:T(8,128)(2,1)} %get-tuple-element.53.mixed, bf16[384,1088]{1,0:T(8,128)(2,1)} %get-tuple-element.54.whole.out_w, f32[16,1088]{1,0:T(8,128)} %get-tuple-element.55.vecs), custom_call_target="tpu_custom_call" | custom-call | tf_op jit(solution)/shard_map/out_project/pallas_call | solution.py:1103
  128.7 0.8 copy-done.5
  129.5 81.0 %feed.1 = (bf16[400,1088]{1,0:T(8,128)(2,1)}, bf16[400,1088]{1,0:T(8,128)(2,1)}, bf16[400,1088]{1,0:T(8,128)(2,1)}, f32[256,1088]{1,0:T(8,128)}, f32[256,1088]{1...) custom-call(f32[256,1088]{1,0:T(8,128)} %out_project.1.middle, ...), custom_call_target="tpu_custom_call" | custom-call | tf_op jit(solution)/shard_map/feed/pallas_call | solution.py:1335
  210.5 0.5 collective-permute-start.3
  211.0 1.6 collective-permute-start.4
  212.6 1.5 collective-permute-start.5
  214.1 35.3 %attend_back.1 = (bf16[4,256,384]{2,1,0:T(8,128)(2,1)}, bf16[8,256,384]{2,1,0:T(8,128)(2,1)}, bf16[8,256,384]{2,1,0:T(8,128)(2,1)}) custom-call(s32[5]{0:T(128)} %bitcast.23, s32[1]{0:T(128)} %bitcast.5.parity, bf16[4,256,384]{2,1,0:T(8,128)(2,1)} %get-tuple-element.50.q, bf16[8,256,384]{2,1,0:T(8,128)(2,1)} %get-tuple-element.51.k, ...), custom_call_target="tpu_custom_call" | custom-call | flops 10000000000 | bytes 9000000 | tf_op jit(solution)/shard_map/attend_back/pallas_call | solution.py:1045
  249.4 4.1 %collective-permute-done.4.from_y = bf16[400,1088]{1,0:T(8,128)(2,1)} collective-permute-done((bf16[400,1088]{1,0:T(8,128)(2,1)}, bf16[400,1088]{1,0:T(8,128)(2,1)}, u32[]{:S(2)}, u32[]{:S(2)}) %collective-permute-start.4) | collective-permute-done | bytes 870432 | tf_op jit(solution)/shard_map/ppermute | solution.py:1731
  253.6 71.8 %back.1 = (bf16[1088,256]{1,0:T(8,128)(2,1)}, f32[1088,256]{1,0:T(8,128)}, bf16[272,4352]{1,0:T(8,128)(2,1)}, bf16[1088,1088]{1,0:T(8,128)(2,1)}, bf16[272,3264]...) custom-call(bf16[256,1088]{1,0:T(8,128)(2,1)} %get-tuple-element.49.x, ...), custom_call_target="tpu_custom_call" | custom-call | tf_op jit(solution)/shard_map/back/pallas_call | solution.py:1674
  325.3 1.4 slice_reduce_fusion
  326.8 1.6 slice_reduce_fusion.1
  328.4 2.2 convert_element_type.13
  330.6 2.1 convert_element_type.12
  332.7 0.7 copy-done.1
  333.4 2.5 convert_element_type.14
  336.2 2.6 convert_element_type.15
  338.8 0.8 copy.33
  339.6 0.6 copy-done.3
  340.3 1.0 copy.34
  (22 shorter events, 0.6 us)
Async XLA Ops:
  7.2 121.5 %all-gather.3.cloned.1.call-start = ((), (), s32[]{:S(2)}) async-start(), calls=%async_computation.2 | async-start | bytes 3502080 | tf_op jit(solution)/shard_map/all_gather | solution.py:1728
  58.4 195.1 %reduce-scatter.2.cloned.1.call-start = ((), (), s32[]{:S(2)}) async-start(), calls=%async_computation.1 | async-start | bytes 1843200 | tf_op jit(solution)/shard_map/reduce_scatter | solution.py:1741
  58.7 70.0 %collective-permute-start.2 = (bf16[264,1088]{1,0:T(8,128)(2,1)}, bf16[264,1088]{1,0:T(8,128)(2,1)S(1)}, u32[]{:S(2)}, u32[]{:S(2)}) collective-permute-start(bf16[264,1088]{1,0:T(8,128)(2,1)} %get-tuple-element.56.cot), channel_id=1, source_target_pairs={{0,24},{4,28},{8,16},{12,20},{16,8},{20,12},{24,0},{28,4},{1,25},{... | collective-permute-start | bytes 1723400 | tf_op jit(solution)/shard_map/ppermute | solution.py:1731
  61.2 67.5 %collective-permute-start.1 = (bf16[264,1088]{1,0:T(8,128)(2,1)}, bf16[264,1088]{1,0:T(8,128)(2,1)}, u32[]{:S(2)}, u32[]{:S(2)}) collective-permute-start(bf16[264,1088]{1,0:T(8,128)(2,1)} %get-tuple-element.56.cot), channel_id=1, source_target_pairs={{0,16},{4,20},{8,24},{12,28},{16,0},{20,4},{24,8},{28,12},{1,17},{... | collective-permute-start | bytes 1723400 | tf_op jit(solution)/shard_map/ppermute | solution.py:1731
  61.7 67.0 %collective-permute-start = (bf16[264,1088]{1,0:T(8,128)(2,1)}, bf16[264,1088]{1,0:T(8,128)(2,1)}, u32[]{:S(2)}, u32[]{:S(2)}) collective-permute-start(bf16[264,1088]{1,0:T(8,128)(2,1)} %get-tuple-element.56.cot), channel_id=1, source_target_pairs={{0,8},{4,12},{8,0},{12,4},{16,24},{20,28},{24,16},{28,20},{1,9},{5... | collective-permute-start | bytes 1723400 | tf_op jit(solution)/shard_map/ppermute | solution.py:1731
  128.7 0.8 copy-start.5
  210.5 38.9 %collective-permute-start.3 = (bf16[400,1088]{1,0:T(8,128)(2,1)}, bf16[400,1088]{1,0:T(8,128)(2,1)S(1)}, u32[]{:S(2)}, u32[]{:S(2)}) collective-permute-start(bf16[400,1088]{1,0:T(8,128)(2,1)} %get-tuple-element.67), channel_id=1, source_target_pairs={{0,8},{4,12},{8,0},{12,4},{16,24},{20,28},{24,16},{28,20},{1,9},{5... | collective-permute-start | bytes 2611208 | tf_op jit(solution)/shard_map/ppermute | solution.py:1731
  211.0 42.5 %collective-permute-start.4 = (bf16[400,1088]{1,0:T(8,128)(2,1)}, bf16[400,1088]{1,0:T(8,128)(2,1)}, u32[]{:S(2)}, u32[]{:S(2)}) collective-permute-start(bf16[400,1088]{1,0:T(8,128)(2,1)} %get-tuple-element.68), channel_id=1, source_target_pairs={{0,16},{4,20},{8,24},{12,28},{16,0},{20,4},{24,8},{28,12},{1,17},{... | collective-permute-start | bytes 2611208 | tf_op jit(solution)/shard_map/ppermute | solution.py:1731
  212.6 40.9 %collective-permute-start.5 = (bf16[400,1088]{1,0:T(8,128)(2,1)}, bf16[400,1088]{1,0:T(8,128)(2,1)}, u32[]{:S(2)}, u32[]{:S(2)}) collective-permute-start(bf16[400,1088]{1,0:T(8,128)(2,1)} %get-tuple-element.69), channel_id=1, source_target_pairs={{0,24},{4,28},{8,16},{12,20},{16,8},{20,12},{24,0},{28,4},{1,25},{... | collective-permute-start | bytes 2611208 | tf_op jit(solution)/shard_map/ppermute | solution.py:1731
  249.4 4.1 %copy-start.4 = (bf16[400,1088]{1,0:T(8,128)(2,1)}, bf16[400,1088]{1,0:T(8,128)(2,1)S(1)}, u32[]{:S(2)}) copy-start(bf16[400,1088]{1,0:T(8,128)(2,1)S(1)} %collective-permute-done.3.from_x) | copy-start | bytes 2611204
  325.3 5.3 %copy-start.2 = (bf16[272,3264]{1,0:T(8,128)(2,1)S(1)}, bf16[272,3264]{1,0:T(8,128)(2,1)}, u32[]{:S(2)}) copy-start(bf16[272,3264]{1,0:T(8,128)(2,1)} %get-tuple-element.78) | copy-start | bytes 5326852
  330.6 2.8 copy-start.1
  333.4 2.8 copy-start
  336.2 2.6 copy-start.6
  338.8 1.4 copy-start.3
Sparse Core Ops, SparseCore 0:
  58.5 57.2 all-gather.2
  210.7 32.9 reduce-scatter.1
where the time goes:
time: 349 us; the launch traced here: 348 us
  Pallas kernels  306 us (88%)
  between operations  14.2 us (4%)
  other arithmetic  9.35 us (3%)
  starting transfers between devices  7.37 us (2%)
  local copies, waits for them, and re-layouts  7.32 us (2%)
  waiting for transfers between devices  4.19 us (1%)
    pallas_call x1, Pallas kernels, feed(): pl.pallas_call(feed_kernel, out_shape=(mixture, mixture, mixture, jax.Sha...  81 us
    pallas_call x1, Pallas kernels, back(): pl.pallas_call(back_kernel, out_shape=(jax.ShapeDtypeStruct((D, ROWS), BF...  71.8 us
    pallas_call x1, Pallas kernels, project(): pl.pallas_call(project_kernel, out_shape=(blocks, keys, keys, jax.ShapeDt...  51.2 us
    pallas_call x1, Pallas kernels, attend_back(): pl.pallas_call(attend_back_kernel, out_shape=(jax.ShapeDtypeStruct((CHIPS...  35.3 us
    pallas_call x1, Pallas kernels, attend(): pl.pallas_call(attend_kernel, out_shape=(jax.ShapeDtypeStruct((CHIPS, ROW...  34.7 us
    pallas_call x1, Pallas kernels, out_project(): pl.pallas_call(out_kernel, out_shape=jax.ShapeDtypeStruct((ROWS, D), F32)...  31.8 us
    convert_element_type x4, other arithmetic, plane_device(): array.astype(F32)  9.35 us
    ppermute x6, starting transfers between devices, from_chips(): lax.ppermute(array, 'ctx', list(enumerate(to)))  7.11 us
  transfers between devices with their start and end apart: 8, of which 1 were waited for; matrix products, arithmetic and copies ran while one was open for 0% of the time, Pallas kernels for 29%

commit v1 on v0

--- a/solution.py
+++ b/solution.py
@@ -1419,11 +1419,6 @@
     downs.start()
     outs = ZScatter(e, g_out, s_out, zo_right, zo_left, z_send.at[0], z_recv.at[0])
     outs.begin()
-    result = out_own[...]
-    for ref in (from_x, from_y, from_far):
-        result = result + ref[:ROWS].astype(F32)
-    output[...] = result.T.astype(BF16)
-    normed, inverse = normalize(x[...].astype(F32))
     local[...] = jnp.zeros_like(local)
     for k in range(CHIPS):
         joint[k, :, :WIDE] = dq[k]
@@ -1523,21 +1518,21 @@
     hand(1, own_out, all_out, 0).start()
     summed.relay()
     weights.second()
+    others.forward()
+    weights.last(own_qkv)
+    qkvs = spread(1, own_qkv, all_qkv, 144, 80)
+    qkvs.start()
+    hand(2, own_qkv, all_qkv, 0).start()
+    all_qkv[p, t] = own_qkv[...]
+    normed, inverse = normalize(x[...].astype(F32))
     total = rows_own[...] + summed.total()
-    grad_x[...] = (grad_mid[...] + norm_back(total, normed, inverse, vecs[GAIN_1 : GAIN_1 + 1])).T
     local[:4] = sums[:4]
     local[4:5] = jnp.sum(total * normed, 0, keepdims=True)
     local[5:6] = jnp.sum(total, 0, keepdims=True)
     local[pl.ds(8 + t, 1), :] = up_sum[...]
     twin = remote(local, vec_land.at[0], v_send.at[0], v_recv.at[0], e.twin())
     twin.start()
-    others.forward()
-    others.have_x()
-    others.have_y()
-    hand(1, own_out, all_out, 1).start()
-    hand(1, own_out, all_out, 2).start()
-    others.have_far()
-    hand(1, own_out, all_out, 3).start()
+    grad_x[...] = (grad_mid[...] + norm_back(total, normed, inverse, vecs[GAIN_1 : GAIN_1 + 1])).T
     twin.wait()
     totals[...] = local[...] + vec_land[0]
     planes = [
@@ -1545,11 +1540,34 @@
     ]
     for copy in planes:
         copy.start()
-    weights.last(own_qkv)
-    qkvs = spread(1, own_qkv, all_qkv, 144, 80)
-    qkvs.start()
-    hand(2, own_qkv, all_qkv, 0).start()
-    all_qkv[p, t] = own_qkv[...]
+    qkvs.forward()
+    others.have_x()
+    others.have_y()
+    hand(1, own_out, all_out, 1).start()
+    hand(1, own_out, all_out, 2).start()
+    others.have_far()
+    hand(1, own_out, all_out, 3).start()
+    handed(0, share, all_up)
+    for copy in keeps:
+        copy.wait()
+
+    def lay_up(q, carry):
+        rows = rows16(q * TILE, 144)
+        for s in range(CHIPS):
+            for i in range(4):
+                column = D * i + HEAD_DIM * (i % 2) + 256 * s
+                up_out[rows, column : column + 256] = all_up[q, s, :, 256 * i : 256 * (i + 1)]
+        for s in range(0, CHIPS, 2):
+            pair = [all_up[q, s + i, :, 1024:].astype(F32) for i in range(2)]
+            column = D * s + 1024
+            up_out[rows, column : column + TILE] = jnp.concatenate(pair, 1).astype(BF16)
+        return carry
+
+    lax.fori_loop(0, 2, lay_up, 0)
+    qkvs.have_x()
+    hand(2, own_qkv, all_qkv, 1).start()
+    qkvs.have_y()
+    hand(2, own_qkv, all_qkv, 2).start()
     for copy in planes:
         copy.wait()
     local[...] = totals[...] + vec_land[1] + vec_land[2] + vec_land[3]
@@ -1559,26 +1577,18 @@
     ]
     for copy in chips:
         copy.start()
-
-    handed(0, share, all_up)
+    qkvs.have_far()
+    hand(2, own_qkv, all_qkv, 3).start()
+
+    result = out_own[...]
+    for ref in (from_x, from_y, from_far):
+        result = result + ref[:ROWS].astype(F32)
+    output[...] = result.T.astype(BF16)
     handed(3, share_down, all_down)
-    for copy in keeps:
-        copy.wait()
-    for s in range(CHIPS):
-        for q in range(2):
-            rows = slice(q * TILE, q * TILE + 144)
-            for i in range(4):
-                column = D * i + HEAD_DIM * (i % 2) + 256 * s
-                up_out[rows, column : column + 256] = all_up[q, s, :, 256 * i : 256 * (i + 1)]
+    for q in range(2):
+        for s in range(CHIPS):
             down_out[rows16(z % 2 * 64 + 256 * s + TILE * q, TILE)] = all_down[q, s, :TILE]
-    for q in range(2):
-        rows = slice(q * TILE, q * TILE + 144)
-        for s in range(0, CHIPS, 2):
-            pair = [all_up[q, s + i, :, 1024:].astype(F32) for i in range(2)]
-            column = D * s + 1024
-            up_out[rows, column : column + TILE] = jnp.concatenate(pair, 1).astype(BF16)
         down_out[rows16((1 - z % 2) * 1024 + 32 * q, 32)] = all_down[q, z, TILE:]
-
     handed(1, own_out, all_out)
     ahead = (CHIPS - z) % CHIPS * 16
     for s in range(CHIPS - 1):
@@ -1596,13 +1606,6 @@
         def _():
             o_out[192 + 16 * u : 208 + 16 * u] = strip
 
-    qkvs.forward()
-    qkvs.have_x()
-    qkvs.have_y()
-    hand(2, own_qkv, all_qkv, 1).start()
-    hand(2, own_qkv, all_qkv, 2).start()
-    qkvs.have_far()
-    hand(2, own_qkv, all_qkv, 3).start()
     for copy in chips:
         copy.wait()
     totals[...] = local[...] + vec_land[4] + vec_land[5] + vec_land[6]
@@ -1646,8 +1649,9 @@
             if head >= 0:
                 for a in range(3):
                     source[a * HEADS + head] = (s, a * WIDE + slot * HEAD_DIM)
-    for q in range(2):
-        rows = slice(q * TILE, q * TILE + 144)
+
+    def lay_qkv(q, carry):
+        rows = rows16(q * TILE, 144)
 
         def piece(g, side):
             s, column = source[g]
@@ -1660,6 +1664,9 @@
             qkv_out[rows, column : column + TILE] = jnp.where(left, piece(g, 0), piece(g + 1, 1)).astype(BF16)
         column = (3 * HEADS - 1) * HEAD_DIM
         qkv_out[rows, column : column + HEAD_DIM] = piece(3 * HEADS - 1, 0)[:, :HEAD_DIM].astype(BF16)
+        return carry
+
+    lax.fori_loop(0, 2, lay_qkv, 0)
     for user in (downs, others, qkvs, summed):
         user.sent()
 

time: 349 us -> 343 us (0.983)
  Pallas kernels: 306 us -> 300 us
    pallas_call x1, Pallas kernels: 71.8 us -> 65.9 us  [back(): pl.pallas_call(back_kernel, out_shape=(jax.ShapeDtypeStruct((D, ROWS), BF...]
  transfers between devices with their start and end apart: 8 -> 8, of which waited for: 1 -> 1; matrix products, arithmetic and copies ran while one was open for 0% -> 0% of each run, Pallas kernels for 29% -> 30%
where the time goes in v1:
time: 343 us; the launch traced here: 342 us
  Pallas kernels  300 us (87%)
  between operations  14.2 us (4%)
  other arithmetic  9.35 us (3%)
  starting transfers between devices  7.37 us (2%)
  local copies, waits for them, and re-layouts  7.32 us (2%)
  waiting for transfers between devices  4.19 us (1%)
    pallas_call x1, Pallas kernels, feed(): pl.pallas_call(feed_kernel, out_shape=(mixture, mixture, mixture, jax.Sha...  81 us
    pallas_call x1, Pallas kernels, back(): pl.pallas_call(back_kernel, out_shape=(jax.ShapeDtypeStruct((D, ROWS), BF...  65.9 us
    pallas_call x1, Pallas kernels, project(): pl.pallas_call(project_kernel, out_shape=(blocks, keys, keys, jax.ShapeDt...  51.2 us
    pallas_call x1, Pallas kernels, attend_back(): pl.pallas_call(attend_back_kernel, out_shape=(jax.ShapeDtypeStruct((CHIPS...  35.3 us
    pallas_call x1, Pallas kernels, attend(): pl.pallas_call(attend_kernel, out_shape=(jax.ShapeDtypeStruct((CHIPS, ROW...  34.7 us
    pallas_call x1, Pallas kernels, out_project(): pl.pallas_call(out_kernel, out_shape=jax.ShapeDtypeStruct((ROWS, D), F32)...  31.8 us
    convert_element_type x4, other arithmetic, plane_device(): array.astype(F32)  9.35 us
    ppermute x6, starting transfers between devices, from_chips(): lax.ppermute(array, 'ctx', list(enumerate(to)))  7.11 us
  transfers between devices with their start and end apart: 8, of which 1 were waited for; matrix products, arithmetic and copies ran while one was open for 0% of the time, Pallas kernels for 30%

profile of v1, /device:TPU:0, one launch (start us, length us, event | category | flops | bytes accessed | tf_op | source)
XLA Modules:
  0.0 342.3 jit_solution(8534239471446790708)
XLA Ops:
  7.2 51.2 %project.1 = (bf16[4,256,384]{2,1,0:T(8,128)(2,1)}, bf16[8,256,384]{2,1,0:T(8,128)(2,1)}, bf16[8,256,384]{2,1,0:T(8,128)(2,1)}, bf16[4,256,1088]{2,1,0:T(8,128)(...) custom-call(bf16[1088,256]{1,0:T(8,128)(2,1)} %bitcast.19, ...), custom_call_target="tpu_custom_call" | custom-call | tf_op jit(solution)/shard_map/project/pallas_call | solution.py:823
  58.7 2.5 collective-permute-start.2
  61.2 0.5 collective-permute-start.1
  61.7 0.5 collective-permute-start
  62.2 34.7 %attend.1 = (bf16[4,256,384]{2,1,0:T(8,128)(2,1)}, f32[3,8,256]{2,1,0:T(8,128)}) custom-call(s32[5]{0:T(128)} %bitcast.22, s32[1]{0:T(128)} %bitcast.5.parity, bf16[4,256,384]{2,1,0:T(8,128)(2,1)} %get-tuple-element.50.q, bf16[8,256,384]{2,1,0:T(8,128)(2,1)} %get-tuple-element.51.k, bf16[8,256,384]{2,1,0:T(8,128)(2,1)} %get-tuple-element.52.v), custom_call_target="tpu_custom_call" | custom-call | flops 4000000000 | bytes 5000000 | tf_op jit(solution)/shard_map/attend/pallas_call | solution.py:953
  96.9 31.8 %out_project.1.middle = f32[256,1088]{1,0:T(8,128)} custom-call(bf16[256,1088]{1,0:T(8,128)(2,1)} %get-tuple-element.49.x, bf16[4,256,384]{2,1,0:T(8,128)(2,1)} %get-tuple-element.53.mixed, bf16[384,1088]{1,0:T(8,128)(2,1)} %get-tuple-element.54.whole.out_w, f32[16,1088]{1,0:T(8,128)} %get-tuple-element.55.vecs), custom_call_target="tpu_custom_call" | custom-call | tf_op jit(solution)/shard_map/out_project/pallas_call | solution.py:1103
  128.7 0.8 copy-done.5
  129.5 81.0 %feed.1 = (bf16[400,1088]{1,0:T(8,128)(2,1)}, bf16[400,1088]{1,0:T(8,128)(2,1)}, bf16[400,1088]{1,0:T(8,128)(2,1)}, f32[256,1088]{1,0:T(8,128)}, f32[256,1088]{1...) custom-call(f32[256,1088]{1,0:T(8,128)} %out_project.1.middle, ...), custom_call_target="tpu_custom_call" | custom-call | tf_op jit(solution)/shard_map/feed/pallas_call | solution.py:1335
  210.5 0.5 collective-permute-start.3
  211.0 1.6 collective-permute-start.4
  212.6 1.5 collective-permute-start.5
  214.1 35.3 %attend_back.1 = (bf16[4,256,384]{2,1,0:T(8,128)(2,1)}, bf16[8,256,384]{2,1,0:T(8,128)(2,1)}, bf16[8,256,384]{2,1,0:T(8,128)(2,1)}) custom-call(s32[5]{0:T(128)} %bitcast.23, s32[1]{0:T(128)} %bitcast.5.parity, bf16[4,256,384]{2,1,0:T(8,128)(2,1)} %get-tuple-element.50.q, bf16[8,256,384]{2,1,0:T(8,128)(2,1)} %get-tuple-element.51.k, ...), custom_call_target="tpu_custom_call" | custom-call | flops 10000000000 | bytes 9000000 | tf_op jit(solution)/shard_map/attend_back/pallas_call | solution.py:1045
  249.4 4.1 %collective-permute-done.4.from_y = bf16[400,1088]{1,0:T(8,128)(2,1)} collective-permute-done((bf16[400,1088]{1,0:T(8,128)(2,1)}, bf16[400,1088]{1,0:T(8,128)(2,1)}, u32[]{:S(2)}, u32[]{:S(2)}) %collective-permute-start.4) | collective-permute-done | bytes 870432 | tf_op jit(solution)/shard_map/ppermute | solution.py:1738
  253.6 65.9 %back.1 = (bf16[1088,256]{1,0:T(8,128)(2,1)}, f32[1088,256]{1,0:T(8,128)}, bf16[272,4352]{1,0:T(8,128)(2,1)}, bf16[1088,1088]{1,0:T(8,128)(2,1)}, bf16[272,3264]...) custom-call(bf16[256,1088]{1,0:T(8,128)(2,1)} %get-tuple-element.49.x, ...), custom_call_target="tpu_custom_call" | custom-call | tf_op jit(solution)/shard_map/back/pallas_call | solution.py:1681
  319.5 1.4 slice_reduce_fusion
  320.9 1.6 slice_reduce_fusion.1
  322.6 2.2 convert_element_type.13
  324.8 2.1 convert_element_type.12
  326.8 0.7 copy-done.1
  327.6 2.5 convert_element_type.14
  330.4 2.6 convert_element_type.15
  333.0 0.8 copy.33
  333.8 0.6 copy-done.3
  334.4 1.0 copy.34
  (22 shorter events, 0.6 us)
Async XLA Ops:
  7.2 121.5 %all-gather.3.cloned.1.call-start = ((), (), s32[]{:S(2)}) async-start(), calls=%async_computation.2 | async-start | bytes 3502080 | tf_op jit(solution)/shard_map/all_gather | solution.py:1735
  58.4 195.1 %reduce-scatter.2.cloned.1.call-start = ((), (), s32[]{:S(2)}) async-start(), calls=%async_computation.1 | async-start | bytes 1843200 | tf_op jit(solution)/shard_map/reduce_scatter | solution.py:1748
  58.7 70.0 %collective-permute-start.2 = (bf16[264,1088]{1,0:T(8,128)(2,1)}, bf16[264,1088]{1,0:T(8,128)(2,1)S(1)}, u32[]{:S(2)}, u32[]{:S(2)}) collective-permute-start(bf16[264,1088]{1,0:T(8,128)(2,1)} %get-tuple-element.56.cot), channel_id=1, source_target_pairs={{0,24},{4,28},{8,16},{12,20},{16,8},{20,12},{24,0},{28,4},{1,25},{... | collective-permute-start | bytes 1723400 | tf_op jit(solution)/shard_map/ppermute | solution.py:1738
  61.2 67.5 %collective-permute-start.1 = (bf16[264,1088]{1,0:T(8,128)(2,1)}, bf16[264,1088]{1,0:T(8,128)(2,1)}, u32[]{:S(2)}, u32[]{:S(2)}) collective-permute-start(bf16[264,1088]{1,0:T(8,128)(2,1)} %get-tuple-element.56.cot), channel_id=1, source_target_pairs={{0,16},{4,20},{8,24},{12,28},{16,0},{20,4},{24,8},{28,12},{1,17},{... | collective-permute-start | bytes 1723400 | tf_op jit(solution)/shard_map/ppermute | solution.py:1738
  61.7 67.0 %collective-permute-start = (bf16[264,1088]{1,0:T(8,128)(2,1)}, bf16[264,1088]{1,0:T(8,128)(2,1)}, u32[]{:S(2)}, u32[]{:S(2)}) collective-permute-start(bf16[264,1088]{1,0:T(8,128)(2,1)} %get-tuple-element.56.cot), channel_id=1, source_target_pairs={{0,8},{4,12},{8,0},{12,4},{16,24},{20,28},{24,16},{28,20},{1,9},{5... | collective-permute-start | bytes 1723400 | tf_op jit(solution)/shard_map/ppermute | solution.py:1738
  128.7 0.8 copy-start.5
  210.5 38.9 %collective-permute-start.3 = (bf16[400,1088]{1,0:T(8,128)(2,1)}, bf16[400,1088]{1,0:T(8,128)(2,1)S(1)}, u32[]{:S(2)}, u32[]{:S(2)}) collective-permute-start(bf16[400,1088]{1,0:T(8,128)(2,1)} %get-tuple-element.67), channel_id=1, source_target_pairs={{0,8},{4,12},{8,0},{12,4},{16,24},{20,28},{24,16},{28,20},{1,9},{5... | collective-permute-start | bytes 2611208 | tf_op jit(solution)/shard_map/ppermute | solution.py:1738
  211.0 42.5 %collective-permute-start.4 = (bf16[400,1088]{1,0:T(8,128)(2,1)}, bf16[400,1088]{1,0:T(8,128)(2,1)}, u32[]{:S(2)}, u32[]{:S(2)}) collective-permute-start(bf16[400,1088]{1,0:T(8,128)(2,1)} %get-tuple-element.68), channel_id=1, source_target_pairs={{0,16},{4,20},{8,24},{12,28},{16,0},{20,4},{24,8},{28,12},{1,17},{... | collective-permute-start | bytes 2611208 | tf_op jit(solution)/shard_map/ppermute | solution.py:1738
  212.6 40.9 %collective-permute-start.5 = (bf16[400,1088]{1,0:T(8,128)(2,1)}, bf16[400,1088]{1,0:T(8,128)(2,1)}, u32[]{:S(2)}, u32[]{:S(2)}) collective-permute-start(bf16[400,1088]{1,0:T(8,128)(2,1)} %get-tuple-element.69), channel_id=1, source_target_pairs={{0,24},{4,28},{8,16},{12,20},{16,8},{20,12},{24,0},{28,4},{1,25},{... | collective-permute-start | bytes 2611208 | tf_op jit(solution)/shard_map/ppermute | solution.py:1738
  249.4 4.1 %copy-start.4 = (bf16[400,1088]{1,0:T(8,128)(2,1)}, bf16[400,1088]{1,0:T(8,128)(2,1)S(1)}, u32[]{:S(2)}) copy-start(bf16[400,1088]{1,0:T(8,128)(2,1)S(1)} %collective-permute-done.3.from_x) | copy-start | bytes 2611204
  319.5 5.3 %copy-start.2 = (bf16[272,3264]{1,0:T(8,128)(2,1)S(1)}, bf16[272,3264]{1,0:T(8,128)(2,1)}, u32[]{:S(2)}) copy-start(bf16[272,3264]{1,0:T(8,128)(2,1)} %get-tuple-element.78) | copy-start | bytes 5326852
  324.8 2.8 copy-start.1
  327.6 2.8 copy-start
  330.4 2.6 copy-start.6
  333.0 1.4 copy-start.3
Sparse Core Ops, SparseCore 0:
  58.5 57.2 all-gather.2
  210.7 32.9 reduce-scatter.1

commit v2 on v1

--- a/solution.py
+++ b/solution.py
@@ -758,6 +758,7 @@
     vecs[8:] = total
     chain.step(3)
     into.wait(half)
+    chain_o.step(1)
 
     def block(k, carry):
         src = e.flip((k + 1) // 2 % 2, k // 2)
@@ -784,12 +785,18 @@
         remote(
             v_out.at[mine], v_out.at[mine], kv_send.at[k + CHIPS], kv_recv.at[k + CHIPS], e.twin()
         ).start()
+
+        @pl.when(k == 1)
+        def _():
+            chain_o.step(2)
+
+        @pl.when(k == 3)
+        def _():
+            chain_o.step(3)
+
         return carry
 
     lax.fori_loop(0, CHIPS, block, 0)
-    chain_o.step(1)
-    chain_o.step(2)
-    chain_o.step(3)
     into_o.wait(half_o)
 
     @pl.when(t == CHIPS - 1)

time: 343 us -> 343 us (level)
  no operation moved by 1% of the time
where the time goes in v2:
time: 343 us
  Pallas kernels  299 us (87%)
  between operations  14.2 us (4%)
  other arithmetic  9.35 us (3%)
  starting transfers between devices  7.37 us (2%)
  local copies, waits for them, and re-layouts  7.32 us (2%)
  waiting for transfers between devices  5.46 us (2%)
    pallas_call x1, Pallas kernels, feed(): pl.pallas_call(feed_kernel, out_shape=(mixture, mixture, mixture, jax.Sha...  81.6 us
    pallas_call x1, Pallas kernels, back(): pl.pallas_call(back_kernel, out_shape=(jax.ShapeDtypeStruct((D, ROWS), BF...  64.8 us
    pallas_call x1, Pallas kernels, project(): pl.pallas_call(project_kernel, out_shape=(blocks, keys, keys, jax.ShapeDt...  51.2 us
    pallas_call x1, Pallas kernels, attend_back(): pl.pallas_call(attend_back_kernel, out_shape=(jax.ShapeDtypeStruct((CHIPS...  35.2 us
    pallas_call x1, Pallas kernels, attend(): pl.pallas_call(attend_kernel, out_shape=(jax.ShapeDtypeStruct((CHIPS, ROW...  34.7 us
    pallas_call x1, Pallas kernels, out_project(): pl.pallas_call(out_kernel, out_shape=jax.ShapeDtypeStruct((ROWS, D), F32)...  31.6 us
    convert_element_type x4, other arithmetic, plane_device(): array.astype(F32)  9.35 us
    ppermute x6, starting transfers between devices, from_chips(): lax.ppermute(array, 'ctx', list(enumerate(to)))  7.11 us
  transfers between devices with their start and end apart: 8, of which 1 were waited for; matrix products, arithmetic and copies ran while one was open for 0% of the time, Pallas kernels for 30%

profile of v2, /device:TPU:0, one launch (start us, length us, event | category | flops | bytes accessed | tf_op | source)
XLA Modules:
  0.0 342.9 jit_solution(6232070619509073563)
XLA Ops:
  7.2 51.2 %project.1 = (bf16[4,256,384]{2,1,0:T(8,128)(2,1)}, bf16[8,256,384]{2,1,0:T(8,128)(2,1)}, bf16[8,256,384]{2,1,0:T(8,128)(2,1)}, bf16[4,256,1088]{2,1,0:T(8,128)(...) custom-call(bf16[1088,256]{1,0:T(8,128)(2,1)} %bitcast.19, ...), custom_call_target="tpu_custom_call" | custom-call | tf_op jit(solution)/shard_map/project/pallas_call | solution.py:830
  58.7 2.7 collective-permute-start.2
  61.4 0.3 collective-permute-start.1
  61.7 0.5 collective-permute-start
  62.3 34.7 %attend.1 = (bf16[4,256,384]{2,1,0:T(8,128)(2,1)}, f32[3,8,256]{2,1,0:T(8,128)}) custom-call(s32[5]{0:T(128)} %bitcast.22, s32[1]{0:T(128)} %bitcast.5.parity, bf16[4,256,384]{2,1,0:T(8,128)(2,1)} %get-tuple-element.50.q, bf16[8,256,384]{2,1,0:T(8,128)(2,1)} %get-tuple-element.51.k, bf16[8,256,384]{2,1,0:T(8,128)(2,1)} %get-tuple-element.52.v), custom_call_target="tpu_custom_call" | custom-call | flops 4000000000 | bytes 5000000 | tf_op jit(solution)/shard_map/attend/pallas_call | solution.py:960
  97.0 31.6 %out_project.1.middle = f32[256,1088]{1,0:T(8,128)} custom-call(bf16[256,1088]{1,0:T(8,128)(2,1)} %get-tuple-element.49.x, bf16[4,256,384]{2,1,0:T(8,128)(2,1)} %get-tuple-element.53.mixed, bf16[384,1088]{1,0:T(8,128)(2,1)} %get-tuple-element.54.whole.out_w, f32[16,1088]{1,0:T(8,128)} %get-tuple-element.55.vecs), custom_call_target="tpu_custom_call" | custom-call | tf_op jit(solution)/shard_map/out_project/pallas_call | solution.py:1110
  128.7 0.8 copy-done.5
  129.4 81.6 %feed.1 = (bf16[400,1088]{1,0:T(8,128)(2,1)}, bf16[400,1088]{1,0:T(8,128)(2,1)}, bf16[400,1088]{1,0:T(8,128)(2,1)}, f32[256,1088]{1,0:T(8,128)}, f32[256,1088]{1...) custom-call(f32[256,1088]{1,0:T(8,128)} %out_project.1.middle, ...), custom_call_target="tpu_custom_call" | custom-call | tf_op jit(solution)/shard_map/feed/pallas_call | solution.py:1342
  211.1 1.6 collective-permute-start.3
  212.8 0.5 collective-permute-start.4
  213.2 1.4 collective-permute-start.5
  214.7 35.2 %attend_back.1 = (bf16[4,256,384]{2,1,0:T(8,128)(2,1)}, bf16[8,256,384]{2,1,0:T(8,128)(2,1)}, bf16[8,256,384]{2,1,0:T(8,128)(2,1)}) custom-call(s32[5]{0:T(128)} %bitcast.23, s32[1]{0:T(128)} %bitcast.5.parity, bf16[4,256,384]{2,1,0:T(8,128)(2,1)} %get-tuple-element.50.q, bf16[8,256,384]{2,1,0:T(8,128)(2,1)} %get-tuple-element.51.k, ...), custom_call_target="tpu_custom_call" | custom-call | flops 10000000000 | bytes 9000000 | tf_op jit(solution)/shard_map/attend_back/pallas_call | solution.py:1052
  249.9 5.4 %collective-permute-done.4.from_y = bf16[400,1088]{1,0:T(8,128)(2,1)} collective-permute-done((bf16[400,1088]{1,0:T(8,128)(2,1)}, bf16[400,1088]{1,0:T(8,128)(2,1)}, u32[]{:S(2)}, u32[]{:S(2)}) %collective-permute-start.4) | collective-permute-done | bytes 870432 | tf_op jit(solution)/shard_map/ppermute | solution.py:1745
  255.3 64.8 %back.1 = (bf16[1088,256]{1,0:T(8,128)(2,1)}, f32[1088,256]{1,0:T(8,128)}, bf16[272,4352]{1,0:T(8,128)(2,1)}, bf16[1088,1088]{1,0:T(8,128)(2,1)}, bf16[272,3264]...) custom-call(bf16[256,1088]{1,0:T(8,128)(2,1)} %get-tuple-element.49.x, ...), custom_call_target="tpu_custom_call" | custom-call | tf_op jit(solution)/shard_map/back/pallas_call | solution.py:1688
  320.1 1.4 slice_reduce_fusion
  321.6 1.6 slice_reduce_fusion.1
  323.2 2.2 convert_element_type.13
  325.4 2.1 convert_element_type.12
  327.5 0.7 copy-done.1
  328.2 2.5 convert_element_type.14
  331.0 2.6 convert_element_type.15
  333.6 0.8 copy.33
  334.4 0.6 copy-done.3
  335.0 1.0 copy.34
  (22 shorter events, 0.6 us)
Async XLA Ops:
  7.2 121.5 %all-gather.3.cloned.1.call-start = ((), (), s32[]{:S(2)}) async-start(), calls=%async_computation.2 | async-start | bytes 3502080 | tf_op jit(solution)/shard_map/all_gather | solution.py:1742
  58.5 196.8 %reduce-scatter.2.cloned.1.call-start = ((), (), s32[]{:S(2)}) async-start(), calls=%async_computation.1 | async-start | bytes 1843200 | tf_op jit(solution)/shard_map/reduce_scatter | solution.py:1755
  58.7 69.9 %collective-permute-start.2 = (bf16[264,1088]{1,0:T(8,128)(2,1)}, bf16[264,1088]{1,0:T(8,128)(2,1)S(1)}, u32[]{:S(2)}, u32[]{:S(2)}) collective-permute-start(bf16[264,1088]{1,0:T(8,128)(2,1)} %get-tuple-element.56.cot), channel_id=1, source_target_pairs={{0,24},{4,28},{8,16},{12,20},{16,8},{20,12},{24,0},{28,4},{1,25},{... | collective-permute-start | bytes 1723400 | tf_op jit(solution)/shard_map/ppermute | solution.py:1745
  61.4 67.2 %collective-permute-start.1 = (bf16[264,1088]{1,0:T(8,128)(2,1)}, bf16[264,1088]{1,0:T(8,128)(2,1)}, u32[]{:S(2)}, u32[]{:S(2)}) collective-permute-start(bf16[264,1088]{1,0:T(8,128)(2,1)} %get-tuple-element.56.cot), channel_id=1, source_target_pairs={{0,16},{4,20},{8,24},{12,28},{16,0},{20,4},{24,8},{28,12},{1,17},{... | collective-permute-start | bytes 1723400 | tf_op jit(solution)/shard_map/ppermute | solution.py:1745
  61.7 66.9 %collective-permute-start = (bf16[264,1088]{1,0:T(8,128)(2,1)}, bf16[264,1088]{1,0:T(8,128)(2,1)}, u32[]{:S(2)}, u32[]{:S(2)}) collective-permute-start(bf16[264,1088]{1,0:T(8,128)(2,1)} %get-tuple-element.56.cot), channel_id=1, source_target_pairs={{0,8},{4,12},{8,0},{12,4},{16,24},{20,28},{24,16},{28,20},{1,9},{5... | collective-permute-start | bytes 1723400 | tf_op jit(solution)/shard_map/ppermute | solution.py:1745
  128.6 0.8 copy-start.5
  211.1 38.7 %collective-permute-start.3 = (bf16[400,1088]{1,0:T(8,128)(2,1)}, bf16[400,1088]{1,0:T(8,128)(2,1)S(1)}, u32[]{:S(2)}, u32[]{:S(2)}) collective-permute-start(bf16[400,1088]{1,0:T(8,128)(2,1)} %get-tuple-element.67), channel_id=1, source_target_pairs={{0,8},{4,12},{8,0},{12,4},{16,24},{20,28},{24,16},{28,20},{1,9},{5... | collective-permute-start | bytes 2611208 | tf_op jit(solution)/shard_map/ppermute | solution.py:1745
  212.8 42.5 %collective-permute-start.4 = (bf16[400,1088]{1,0:T(8,128)(2,1)}, bf16[400,1088]{1,0:T(8,128)(2,1)}, u32[]{:S(2)}, u32[]{:S(2)}) collective-permute-start(bf16[400,1088]{1,0:T(8,128)(2,1)} %get-tuple-element.68), channel_id=1, source_target_pairs={{0,16},{4,20},{8,24},{12,28},{16,0},{20,4},{24,8},{28,12},{1,17},{... | collective-permute-start | bytes 2611208 | tf_op jit(solution)/shard_map/ppermute | solution.py:1745
  213.2 42.0 %collective-permute-start.5 = (bf16[400,1088]{1,0:T(8,128)(2,1)}, bf16[400,1088]{1,0:T(8,128)(2,1)}, u32[]{:S(2)}, u32[]{:S(2)}) collective-permute-start(bf16[400,1088]{1,0:T(8,128)(2,1)} %get-tuple-element.69), channel_id=1, source_target_pairs={{0,24},{4,28},{8,16},{12,20},{16,8},{20,12},{24,0},{28,4},{1,25},{... | collective-permute-start | bytes 2611208 | tf_op jit(solution)/shard_map/ppermute | solution.py:1745
  249.9 5.4 %copy-start.4 = (bf16[400,1088]{1,0:T(8,128)(2,1)}, bf16[400,1088]{1,0:T(8,128)(2,1)S(1)}, u32[]{:S(2)}) copy-start(bf16[400,1088]{1,0:T(8,128)(2,1)S(1)} %collective-permute-done.3.from_x) | copy-start | bytes 2611204
  320.1 5.3 %copy-start.2 = (bf16[272,3264]{1,0:T(8,128)(2,1)S(1)}, bf16[272,3264]{1,0:T(8,128)(2,1)}, u32[]{:S(2)}) copy-start(bf16[272,3264]{1,0:T(8,128)(2,1)} %get-tuple-element.78) | copy-start | bytes 5326852
  325.4 2.8 copy-start.1
  328.2 2.8 copy-start
  331.0 2.6 copy-start.6
  333.6 1.4 copy-start.3
Sparse Core Ops, SparseCore 0:
  58.6 59.3 all-gather.2
  211.2 32.4 reduce-scatter.1
